TPU v7x, 128 devices: a whole 4x4x4 slice. The times are simulated.
128 devices in a mesh: guide: 2 (over core), kv: 4 (over y), seq: 16 (over z, x).
Axes of the slice: x: 4, y: 4, z: 4, core: 2. Of those that a mesh axis runs over, the one named last changes fastest.
Arguments:
- hidden: bfloat16 [2, 8, 4608], P(None, None, ('guide', 'seq')), may hold values from -50 to 50
- lengths: int32 [2, 8], replicated, may hold values from 1 to 8192, as said below
- slot_owner: int32 [2, 8], replicated, may hold values from 0 to 7, each once within a row
- allowed_ids: int32 [65536], P(('kv', 'seq')), may hold values from 0 to 131071, as said below
- guidance: float32 [8], replicated, may hold values from 1 to 4
- pre_attn_gain: float32 [4608], P(('guide', 'seq')), may hold values from 0.1 to 1.9
- post_attn_gain: float32 [4608], P(('guide', 'seq')), may hold values from 0.4 to 2.1
- pre_ffw_gain: float32 [4608], P(('guide', 'seq')), may hold values from 0.1 to 1.9
- post_ffw_gain: float32 [4608], P(('guide', 'seq')), may hold values from 0.4 to 2.1
- final_gain: float32 [4608], P(('guide', 'seq')), may hold values from 0.1 to 1.9
- query_weight: bfloat16 [4608, 4096], P(('guide', 'seq'), 'kv'), may hold values from -0.09375 to 0.09375
- key_weight: bfloat16 [4608, 2048], P(('guide', 'seq'), 'kv'), may hold values from -0.09375 to 0.09375
- value_weight: bfloat16 [4608, 2048], P(('guide', 'seq'), 'kv'), may hold values from -0.09375 to 0.09375
- output_weight: bfloat16 [4096, 4608], P('kv', ('guide', 'seq')), may hold values from -1 to 1
- gate_weight: bfloat16 [4608, 36864], P(('guide', 'seq'), 'kv'), may hold values from -1 to 1
- up_weight: bfloat16 [4608, 36864], P(('guide', 'seq'), 'kv'), may hold values from -1 to 1
- down_weight: bfloat16 [36864, 4608], P('kv', ('guide', 'seq')), may hold values from -1 to 1
- embedding: bfloat16 [131072, 4608], P(('kv', 'seq'), 'guide'), may hold values from -1 to 1
- cond_keys: bfloat16 [8, 8192, 2048], P(None, ('guide', 'seq'), 'kv'), may hold values from -6 to 6
- cond_values: bfloat16 [8, 8192, 2048], P(None, ('guide', 'seq'), 'kv'), may hold values from -6 to 6
- uncond_keys: bfloat16 [8, 2048, 2048], P(None, ('guide', 'seq'), 'kv'), may hold values from -6 to 6
- uncond_values: bfloat16 [8, 2048, 2048], P(None, ('guide', 'seq'), 'kv'), may hold values from -6 to 6
Outputs:
- mixed: float32 [8, 65536], P('guide', ('kv', 'seq'))
Inputs may be any that keep to these rules, and one draw needn't show every extreme that they name: lengths[0] lies in 1 to 8192 and some request has exactly 8192; lengths[1] lies in 1 to 2048 and some request has exactly 2048. `slot_owner`: each row is a permutation of the 8 requests. `allowed_ids`: the ids of the i-th aligned block of 1024 entries are distinct and lie in rows i * 2048 to (i + 1) * 2048 - 1 of the table.
All inputs are finite; a program needn't handle non-finite values.
Results may differ from a plain program's by a relative error of at most 0.0039.
Values may be sent and summed in bfloat16 or wider, within the bound.
A program may use at most 128 MiB of HBM per device.

v0:
```python
import jax
import jax.numpy as jnp
from jax import lax
from jax.sharding import PartitionSpec as P

D = 4608
H = 32
HD = 128


EPS = 1e-06
ATTN_CAP = 50.0
LOGIT_CAP = 30.0
THETA = 10000.0
HIGHEST = lax.Precision.HIGHEST


def rotary(values, position):
    half_size = values.shape[-1] // 2
    frequency = THETA ** (-2.0 * jnp.arange(half_size, dtype=jnp.float32) / values.shape[-1])
    angles = position[:, None, None] * frequency
    first_half = values[..., :half_size]
    second_half = values[..., half_size:]
    cosine = jnp.cos(angles)
    sine_part = jnp.sin(angles)
    return jnp.concatenate(
        [
            first_half * cosine - second_half * sine_part,
            second_half * cosine + first_half * sine_part,
        ],
        axis=-1,
    )


def to_slots(slot_pick, array):
    flat = array.astype(jnp.float32).reshape(array.shape[0], array.shape[1], -1)
    moved = jnp.einsum("gsr,gre->gse", slot_pick, flat, precision=HIGHEST)
    return moved.reshape(array.shape).astype(array.dtype)


def to_requests(slot_pick, array):
    flat = array.astype(jnp.float32).reshape(array.shape[0], array.shape[1], -1)
    moved = jnp.einsum("gsr,gse->gre", slot_pick, flat, precision=HIGHEST)
    return moved.reshape(array.shape).astype(array.dtype)


def attend_block(queries, key_block, value_block, slot_len, first_pos, tile_len):
    slot_count, block_len = (key_block.shape[0], key_block.shape[1])
    local_kv, group_size, head_size = (queries.shape[1], queries.shape[2], queries.shape[3])
    live_len = jnp.clip(jnp.max(slot_len) - first_pos, 0, block_len)
    tile_count = (live_len + tile_len - 1) // tile_len

    def one_tile(tile_index, carry):
        numer, denom = carry
        tile_start = tile_index * tile_len
        key_tile = key_block.reshape(slot_count, tile_len, local_kv, head_size)
        value_tile = value_block.reshape(slot_count, tile_len, local_kv, head_size)
        scores = jnp.einsum(
            "rkgd,rtkd->rkgt", queries, key_tile, preferred_element_type=jnp.float32
        )
        places = first_pos + tile_start + jnp.arange(tile_len, dtype=jnp.int32)
        visible = places[None, None, None, :] < slot_len[:, None, None, None]
        probs = jnp.where(visible, jnp.exp(ATTN_CAP * jnp.tanh(scores / ATTN_CAP)), 0.0)
        numer = numer + jnp.einsum(
            "rkgt,rtkd->rkgd",
            probs.astype(jnp.bfloat16),
            value_tile,
            preferred_element_type=jnp.float32,
        )
        denom = denom + jnp.sum(probs, axis=-1)
        return (numer, denom)

    start_numer = jnp.zeros((slot_count, local_kv, group_size, head_size), jnp.float32)
    start_denom = jnp.zeros((slot_count, local_kv, group_size), jnp.float32)
    return lax.fori_loop(0, tile_count, one_tile, (start_numer, start_denom))


def on_device(
    hidden,
    lengths,
    slot_owner,
    allowed_ids,
    guidance,
    pre_attn_gain,
    post_attn_gain,
    pre_ffw_gain,
    post_ffw_gain,
    final_gain,
    query_weight,
    key_weight,
    value_weight,
    output_weight,
    gate_weight,
    up_weight,
    down_weight,
    embedding,
    cond_keys,
    cond_values,
    uncond_keys,
    uncond_values,
):
    kinds, requests, width_local = hidden.shape
    stream_count = kinds * requests
    local_heads = query_weight.shape[1] // HD
    local_kv = key_weight.shape[1] // HD
    group_size = local_heads // local_kv
    streams = hidden.astype(jnp.float32)
    normed = (streams * pre_attn_gain).astype(jnp.bfloat16).reshape(stream_count, width_local)
    query_part = jnp.dot(normed, query_weight, preferred_element_type=jnp.float32)
    key_part = jnp.dot(normed, key_weight, preferred_element_type=jnp.float32)
    value_part = jnp.dot(normed, value_weight, preferred_element_type=jnp.float32)
    square_part = jnp.sum(streams * streams, axis=-1)
    square_sum, query_sum, key_sum, value_sum = lax.psum(
        (square_part, query_part, key_part, value_part), ("guide", "seq")
    )
    row_scale = lax.rsqrt(square_sum / D + EPS).reshape(stream_count, 1)
    position = lengths.astype(jnp.float32).reshape(stream_count)
    queries = (
        rotary((query_sum * row_scale).reshape(stream_count, local_heads, HD), position)
        * (D // H) ** (-0.5)
    ).astype(jnp.bfloat16)
    new_keys = rotary((key_sum * row_scale).reshape(stream_count, local_kv, HD), position).astype(
        jnp.bfloat16
    )
    new_values = (value_sum * row_scale).astype(jnp.bfloat16)
    queries = queries.reshape(kinds, requests, local_kv, group_size, HD)
    new_keys = new_keys.reshape(kinds, requests, local_kv, HD)
    new_values = new_values.reshape(kinds, requests, local_kv, HD)
    matches = slot_owner[:, :, None] == jnp.arange(requests, dtype=jnp.int32)[None, None, :]
    slot_pick = matches.astype(jnp.float32)
    slot_len = jnp.sum(jnp.where(matches, lengths[:, None, :], 0), axis=-1)
    slot_queries = to_slots(slot_pick, queries)
    slot_keys = to_slots(slot_pick, new_keys)
    slot_values = to_slots(slot_pick, new_values)
    guide_index = lax.axis_index("guide")
    seq_index = lax.axis_index("seq")
    block_index = guide_index * lax.axis_size("seq") + seq_index
    cond_len = cond_keys.shape[1]
    uncond_len = uncond_keys.shape[1]
    cond_numer, cond_denom = attend_block(
        slot_queries[0],
        cond_keys,
        cond_values,
        slot_len[0],
        block_index * cond_len,
        min(256, cond_len),
    )
    uncond_numer, uncond_denom = attend_block(
        slot_queries[1],
        uncond_keys,
        uncond_values,
        slot_len[1],
        block_index * uncond_len,
        min(256, uncond_len),
    )
    numer_part = jnp.stack([cond_numer, uncond_numer])
    denom_part = jnp.stack([cond_denom, uncond_denom])
    numer_sum, denom_sum = lax.psum((numer_part, denom_part), ("guide", "seq"))
    own_score = jnp.einsum(
        "gskjd,gskd->gskj", slot_queries, slot_keys, preferred_element_type=jnp.float32
    )
    own_prob = jnp.exp(ATTN_CAP * jnp.tanh(own_score / ATTN_CAP))
    own_weight = own_prob.astype(jnp.bfloat16).astype(jnp.float32)
    numer_total = (
        numer_sum + own_weight[..., None] * slot_values.astype(jnp.float32)[:, :, :, None, :]
    )
    denom_total = denom_sum + own_prob
    attended_slots = (numer_total / denom_total[..., None]).astype(jnp.bfloat16)
    attended = to_requests(slot_pick, attended_slots).reshape(stream_count, local_heads * HD)
    out_part = jnp.dot(attended, output_weight, preferred_element_type=jnp.float32)
    projected = lax.psum(out_part, "kv").reshape(kinds, requests, width_local)
    branch_sq = lax.psum(jnp.sum(projected * projected, axis=-1), ("guide", "seq"))
    out_scale = lax.rsqrt(branch_sq / D + EPS)
    middle = streams + projected * out_scale[..., None] * post_attn_gain
    middle_sq = lax.psum(jnp.sum(middle * middle, axis=-1), ("guide", "seq"))
    ffw_in = (middle * pre_ffw_gain).astype(jnp.bfloat16).reshape(stream_count, width_local)
    ffw_scale = lax.rsqrt(middle_sq / D + EPS).reshape(stream_count, 1)
    gate_part = jnp.dot(ffw_in, gate_weight, preferred_element_type=jnp.float32)
    upward_part = jnp.dot(ffw_in, up_weight, preferred_element_type=jnp.float32)
    gate_sum, upward_sum = lax.psum((gate_part, upward_part), ("guide", "seq"))
    activ = (jax.nn.gelu(gate_sum * ffw_scale, approximate=True) * (upward_sum * ffw_scale)).astype(
        jnp.bfloat16
    )
    down_part = jnp.dot(activ, down_weight, preferred_element_type=jnp.float32)
    ffw_out = lax.psum(down_part, "kv").reshape(kinds, requests, width_local)
    ffw_sq = lax.psum(jnp.sum(ffw_out * ffw_out, axis=-1), ("guide", "seq"))
    branch_scale = lax.rsqrt(ffw_sq / D + EPS)
    last = middle + ffw_out * branch_scale[..., None] * post_ffw_gain
    last_sq = lax.psum(jnp.sum(last * last, axis=-1), ("guide", "seq"))
    final_scale = lax.rsqrt(last_sq / D + EPS)
    final_rows = (last * final_gain).astype(jnp.bfloat16)
    half_rows = lax.all_gather(final_rows, "seq", axis=2, tiled=True)
    table_rows = embedding.shape[0]
    block_first = (lax.axis_index("kv") * lax.axis_size("seq") + seq_index) * table_rows
    picked = jnp.take(embedding, allowed_ids - block_first, axis=0)
    logit_part = jnp.einsum(
        "sd,ad->sa",
        half_rows.reshape(stream_count, half_rows.shape[2]),
        picked,
        preferred_element_type=jnp.float32,
    )
    logit_term = jnp.transpose(logit_part.reshape(kinds, requests, picked.shape[0]), (1, 0, 2))
    logit_share = lax.psum_scatter(logit_term, "guide", scatter_dimension=0, tiled=True)
    half_req = requests // 2
    first_req = guide_index * half_req
    share_scale = jnp.transpose(
        lax.dynamic_slice_in_dim(final_scale, first_req, half_req, 1), (1, 0)
    )
    capped = LOGIT_CAP * jnp.tanh(logit_share * share_scale[:, :, None] / LOGIT_CAP)
    share_weight = lax.dynamic_slice_in_dim(guidance, first_req, half_req, 0)
    return capped[:, 1] + share_weight[:, None] * (capped[:, 0] - capped[:, 1])


def solution(mesh):
    return jax.shard_map(
        on_device,
        mesh=mesh,
        in_specs=(
            P(None, None, ("guide", "seq")),
            P(),
            P(),
            P(("kv", "seq")),
            P(),
            P(("guide", "seq")),
            P(("guide", "seq")),
            P(("guide", "seq")),
            P(("guide", "seq")),
            P(("guide", "seq")),
            P(("guide", "seq"), "kv"),
            P(("guide", "seq"), "kv"),
            P(("guide", "seq"), "kv"),
            P("kv", ("guide", "seq")),
            P(("guide", "seq"), "kv"),
            P(("guide", "seq"), "kv"),
            P("kv", ("guide", "seq")),
            P(("kv", "seq"), "guide"),
            P(None, ("guide", "seq"), "kv"),
            P(None, ("guide", "seq"), "kv"),
            P(None, ("guide", "seq"), "kv"),
            P(None, ("guide", "seq"), "kv"),
        ),
        out_specs=P("guide", ("kv", "seq")),
        check_vma=False,
    )
```

profile of v0, /device:TPU:1, one launch (start us, length us, event | category | flops | bytes accessed | tf_op | source)
XLA Modules:
  0.0 685.3 jit_solution(3180978337750881133)
XLA Ops:
  6.5 1.9 fusion.79
  8.5 0.8 fusion.58
  9.3 0.8 select_reduce_fusion
  10.1 0.7 slice_reduce_fusion.1
  10.8 0.7 convert_element_type.96
  11.5 70.0 %psum.99 = f32[2,8]{1,0:T(2,128)S(1)} all-reduce(f32[2,8]{1,0:T(2,128)S(1)} %fusion.58), channel_id=1, replica_groups=mesh['guide'=2,'kv'=4,'seq'=16] {'guide','seq'}, use_global_device_ids=true, to_apply=%region_4.0 | all-reduce | flops 16 | bytes 128 | tf_op jit(solution)/shard_map/psum | solution.py:113
  81.6 1.7 fusion.75
  83.3 1.7 fusion.77
  86.5 23.5 %all-reduce.9.cloned.1.call-done = f32[16,1024]{1,0:T(8,128)} async-done(((f32[16,1024]{1,0:T(8,128)}), f32[16,1024]{1,0:T(8,128)}) %all-reduce.9.cloned.1.call-update) | async-done | bytes 65552 | tf_op jit(solution)/shard_map/psum | solution.py:113
  110.0 0.9 multiply_bitcast_fusion
  111.1 0.9 convolution_convert_fusion.1
  112.0 2.2 fusion.17
  114.3 2.3 while.28
  114.4 2.0 fusion.127
  116.4 0.2 fusion.128
  116.7 1.4 fusion.39
  118.2 1.6 while.29
  118.3 1.3 convolution_add_fusion.2
  119.9 0.6 pad_maximum_fusion.2
  120.6 0.6 pad_maximum_fusion
  121.3 95.4 %all-reduce.15.cloned.1.call-done = (f32[2,8,4,2]{1,2,3,0:T(4,128)}, f32[16,512]{1,0:T(8,128)}, f32[16,512]{1,0:T(8,128)}) async-done(((f32[2,8,4,2]{1,2,3,0:T(4,128)}, f32[16,512]{1,0:T(8,128)}, f32[16,512]{1,0:T(8,128)}), (f32[2,8,4,2]{1,2,3,0:T(4,128)}, f32[16,512]{1,0:T(8,128)}, f32[16,512]{1,0:T(8,128)})) %all-reduce.15.cloned.1.call-update) | async-done | bytes 66064 | tf_op jit(solution)/shard_map/psum | solution.py:158
  216.7 0.8 broadcast_multiply_fusion
  217.8 0.2 fusion.27
  218.0 0.2 fusion.54
  218.3 1.0 fusion.29
  219.3 0.7 fusion.83
  220.3 93.1 %all-reduce.11.cloned.1.call-done = f32[2,8,4,2,128]{4,3,2,1,0:T(2,128)} async-done(((f32[2,8,4,2,128]{4,3,2,1,0:T(2,128)}), f32[2,8,4,2,128]{4,3,2,1,0:T(2,128)}) %all-reduce.11.cloned.1.call-update) | async-done | bytes 65552 | tf_op jit(solution)/shard_map/psum | solution.py:158
  313.4 1.0 fusion.50
  314.6 0.2 fusion.99
  314.8 13.2 %psum.104 = f32[16,144]{1,0:T(8,128)S(1)} all-reduce(f32[16,144]{1,0:T(8,128)S(1)} %fusion.99), channel_id=1, replica_groups=mesh['guide'=2,'kv'=4,'seq'=16] {'kv'}, use_global_device_ids=true, to_apply=%region_16.17 | all-reduce | flops 2304 | bytes 18432 | tf_op jit(solution)/shard_map/psum | solution.py:171
  328.1 67.2 %psum.105 = f32[2,8]{1,0:T(2,128)S(1)} all-reduce(f32[2,8]{1,0:T(2,128)S(1)} %reduce_sum.83), channel_id=1, replica_groups=mesh['guide'=2,'kv'=4,'seq'=16] {'guide','seq'}, use_global_device_ids=true, to_apply=%region_18.19 | all-reduce | flops 16 | bytes 128 | tf_op jit(solution)/shard_map/psum | solution.py:172
  395.4 0.2 multiply_reduce_fusion.2
  395.5 1.3 fusion.89
  396.8 0.5 copy-done.1
  397.3 1.3 fusion.91
  398.7 14.8 %gather_fusion = bf16[1024,2304]{1,0:T(8,128)(2,1)} fusion(bf16[2048,2304]{1,0:T(8,128)(2,1)} %param.43, s32[1024]{0:T(1024)S(1)} %fusion.88), kind=kCustom, calls=%fused_computation | custom fusion | bytes 9441280 | tf_op jit(solution)/shard_map/jit(_take)/gather | solution.py:195
  413.5 0.6 dynamic-slice
  414.7 62.7 %psum.107 = f32[2,8]{1,0:T(2,128)S(1)} all-reduce(f32[2,8]{1,0:T(2,128)S(1)} %get-tuple-element.260), channel_id=1, replica_groups=mesh['guide'=2,'kv'=4,'seq'=16] {'guide','seq'}, use_global_device_ids=true, to_apply=%region_21.22 | all-reduce | flops 16 | bytes 128 | tf_op jit(solution)/shard_map/psum | solution.py:175
  477.5 21.1 %all-reduce.17.cloned.1.call-done = (f32[16,9216]{1,0:T(8,128)}, f32[16,9216]{1,0:T(8,128)}) async-done(((f32[16,9216]{1,0:T(8,128)}, f32[16,9216]{1,0:T(8,128)}), (f32[16,9216]{1,0:T(8,128)}, f32[16,9216]{1,0:T(8,128)})) %all-reduce.17.cloned.1.call-update) | async-done | bytes 1179664 | tf_op jit(solution)/shard_map/psum | solution.py:180
  498.6 3.0 fusion.42
  501.6 13.1 %psum.109 = f32[16,144]{1,0:T(8,128)S(1)} all-reduce(f32[16,144]{1,0:T(8,128)S(1)} %fusion.42), channel_id=1, replica_groups=mesh['guide'=2,'kv'=4,'seq'=16] {'kv'}, use_global_device_ids=true, to_apply=%region_23.24 | all-reduce | flops 2304 | bytes 18432 | tf_op jit(solution)/shard_map/psum | solution.py:185
  515.0 69.8 %psum.110 = f32[2,8]{1,0:T(2,128)S(1)} all-reduce(f32[2,8]{1,0:T(2,128)S(1)} %reduce_sum.86), channel_id=1, replica_groups=mesh['guide'=2,'kv'=4,'seq'=16] {'guide','seq'}, use_global_device_ids=true, to_apply=%region_25.26 | all-reduce | flops 16 | bytes 128 | tf_op jit(solution)/shard_map/psum | solution.py:186
  584.8 0.2 multiply_reduce_fusion
  585.1 18.4 %all_gather.3 = bf16[2,8,2304]{1,0,2:T(2,128)(2,1)S(1)} all-gather(bf16[2,8,144]{1,0,2:T(2,128)(2,1)S(1)} %copy.69), channel_id=1, replica_groups=mesh['guide'=2,'kv'=4,'seq'=16] {'seq'}, dimensions={2}, use_global_device_ids=true | all-gather | bytes 78336 | tf_op jit(solution)/shard_map/all_gather | solution.py:192
  603.5 4.7 fusion.21
  608.3 68.8 %psum.111 = f32[2,8]{1,0:T(2,128)S(1)} all-reduce(f32[2,8]{1,0:T(2,128)S(1)} %get-tuple-element.266), channel_id=1, replica_groups=mesh['guide'=2,'kv'=4,'seq'=16] {'guide','seq'}, use_global_device_ids=true, to_apply=%region_28.29 | all-reduce | flops 16 | bytes 128 | tf_op jit(solution)/shard_map/psum | solution.py:189
  677.1 0.9 fusion.53
  678.1 0.7 fusion.63
  (81 shorter events, 3.0 us)
Async XLA Ops:
  6.5 389.0 %copy-start = (bf16[144,9216]{1,0:T(8,128)(2,1)S(1)}, bf16[144,9216]{1,0:T(8,128)(2,1)}, u32[]{:S(2)}) copy-start(bf16[144,9216]{1,0:T(8,128)(2,1)} %param.41) | copy-start | bytes 7962628
  6.5 103.4 %all-reduce.9.cloned.1.call-start = ((), (), s32[]{:S(2)}) async-start(), calls=%async_computation | async-start | bytes 131072 | tf_op jit(solution)/shard_map/psum | solution.py:113
  8.5 208.2 %all-reduce.15.cloned.1.call-start = ((), (), s32[]{:S(2)}) async-start(), calls=%async_computation.3 | async-start | bytes 147456 | tf_op jit(solution)/shard_map/psum | solution.py:158
  118.1 99.7 %copy-start.4 = (s32[2,8]{1,0:T(2,128)S(1)}, s32[2,8]{1,0:T(2,128)}, u32[]{:S(2)}) copy-start(s32[2,8]{1,0:T(2,128)} %param.28) | copy-start | bytes 196
  118.1 196.5 %copy-start.2 = (bf16[1024,144]{0,1:T(8,128)(2,1)S(1)}, bf16[1024,144]{0,1:T(8,128)(2,1)}, u32[]{:S(2)}) copy-start(bf16[1024,144]{0,1:T(8,128)(2,1)} %param.39) | copy-start | bytes 884740
  118.1 277.2 %copy-start.3 = (bf16[2,8,144]{2,1,0:T(8,128)(2,1)S(1)}, bf16[2,8,144]{2,1,0:T(8,128)(2,1)}, u32[]{:S(2)}) copy-start(bf16[2,8,144]{2,1,0:T(8,128)(2,1)} %param.26) | copy-start | bytes 13828
  118.2 277.2 %copy-start.7 = (f32[144]{0:T(256)S(1)}, f32[144]{0:T(256)}, u32[]{:S(2)}) copy-start(f32[144]{0:T(256)} %param.32) | copy-start | bytes 1732
  118.2 277.4 %copy-start.6 = (f32[144]{0:T(256)S(1)}, f32[144]{0:T(256)}, u32[]{:S(2)}) copy-start(f32[144]{0:T(256)} %param.33) | copy-start | bytes 1732
  120.5 192.9 %all-reduce.11.cloned.1.call-start = ((), (), s32[]{:S(2)}) async-start(), calls=%async_computation.1 | async-start | bytes 131072 | tf_op jit(solution)/shard_map/psum | solution.py:158
  121.3 377.4 %all-reduce.17.cloned.1.call-start = ((), (), s32[]{:S(2)}) async-start(), calls=%async_computation.4 | async-start | bytes 2359296 | tf_op jit(solution)/shard_map/psum | solution.py:180
  395.3 2.0 copy-start.1
  397.3 1.4 copy-start.5
  398.6 278.5 %all-reduce.13.cloned.1.call-start = ((), (), s32[]{:S(2)}) async-start(), calls=%async_computation.2 | async-start | bytes 131072
  398.7 14.8 %copy-start.11 = (u32[128]{0:T(128)S(1)}, u32[128]{0:T(128)}, u32[]{:S(2)}) copy-start(u32[128]{0:T(128)} %constant.168) | copy-start | bytes 1540
  413.5 101.5 %copy-start.10 = (f32[8]{0:T(128)S(1)}, f32[8]{0:T(128)}, u32[]{:S(2)}) copy-start(f32[8]{0:T(128)} %param.30) | copy-start | bytes 100
  413.5 171.4 %copy-start.8 = (f32[144]{0:T(256)S(1)}, f32[144]{0:T(256)}, u32[]{:S(2)}) copy-start(f32[144]{0:T(256)} %param.34) | copy-start | bytes 1732
  413.5 171.4 %copy-start.9 = (f32[144]{0:T(256)S(1)}, f32[144]{0:T(256)}, u32[]{:S(2)}) copy-start(f32[144]{0:T(256)} %param.35) | copy-start | bytes 1732
Sparse Core Ops, SparseCore 0:
  10.6 99.2 all-reduce.8
  120.6 96.0 all-reduce.14
  220.0 93.3 all-reduce.10
  398.7 99.8 all-reduce.16
  608.4 23.3 all-reduce.12
where the time goes:
time: 686 us; the launch traced here: 685 us
  blocking collectives  383 us (56%)
  waiting for transfers between devices  233 us (34%)
  matrix products  25 us (4%)
  local copies, waits for them, and re-layouts  17.3 us (3%)
  between operations  15.4 us (2%)
  other arithmetic  10.9 us (2%)
    psum x2, waiting for transfers between devices, on_device(): numer_sum, denom_sum = lax.psum((numer_part, denom_part), ('guide', 'seq'))  189 us
    psum x1, blocking collectives, on_device(): lax.psum((square_part, query_part, key_part, value_part), ('guide', 'seq'))  70 us
    psum x1, blocking collectives, on_device(): ffw_sq = lax.psum(jnp.sum(ffw_out * ffw_out, axis=-1), ('guide', 'seq'))  69.8 us
    psum x1, blocking collectives, on_device(): last_sq = lax.psum(jnp.sum(last * last, axis=-1), ('guide', 'seq'))  68.8 us
    psum x1, blocking collectives, on_device(): lax.psum(jnp.sum(projected * projected, axis=-1), ('guide', 'seq'))  67.2 us
    psum x1, blocking collectives, on_device(): middle_sq = lax.psum(jnp.sum(middle * middle, axis=-1), ('guide', 'seq'))  62.7 us
    psum x1, waiting for transfers between devices, on_device(): lax.psum((square_part, query_part, key_part, value_part), ('guide', 'seq'))  23.5 us
    psum x1, waiting for transfers between devices, on_device(): gate_sum, upward_sum = lax.psum((gate_part, upward_part), ('guide', 'seq'))  21.1 us
  transfers between devices with their start and end apart: 5, of which 4 were waited for; matrix products, arithmetic and copies ran while one was open for 4% of the time, Pallas kernels for 0%

commit v1 on v0

v1 whole, which is shorter than its diff:
```python
import jax
import jax.numpy as jnp
from jax import lax
from jax.experimental import pallas as pl
from jax.experimental.pallas import tpu as pltpu
from jax.sharding import PartitionSpec as P

D = 4608
H = 32
HD = 128
EPS = 1e-06
ATTN_CAP = 50.0
LOGIT_CAP = 30.0
THETA = 10000.0
MESH = pl.DeviceIdType.MESH
F32 = jnp.float32
BF16 = jnp.bfloat16
NG, NKV, NS = 2, 4, 16
NP = NG * NS
WL = D // NP
FFL = 9216
FB = 256
EXTRA = 8
ROWS = 2048
HALF = D // 2
PICK = 1024


def iota(shape, dim):
    return lax.broadcasted_iota(jnp.int32, shape, dim)


def column_to_row(col):
    n = col.shape[0]
    spread = jnp.where(iota((n, 128), 0) == iota((n, 128), 1), jnp.broadcast_to(col, (n, 128)), 0.0)
    return jnp.sum(spread, axis=0, keepdims=True)


def row_to_column(row, n, first=0):
    lanes = iota((n, 128), 1)
    picked = jnp.where(lanes == iota((n, 128), 0) + first, jnp.broadcast_to(row, (n, 128)), 0.0)
    return jnp.sum(picked, axis=1, keepdims=True)


def nt_dot(a, b):
    return lax.dot_general(a, b, (((1,), (1,)), ((), ())), preferred_element_type=F32)


def nn_dot(a, b):
    return jnp.dot(a, b, preferred_element_type=F32)


def one_hot(mask):
    return jnp.where(mask, 1.0, 0.0).astype(BF16)


def step_kernel(
    lengths, owner, guidance, hidden, ids, cosine, sine, gains,
    qw_h, kw_h, vw_h, ow_h, gw_h, uw_h, dw_h, emb_h, ck_h, cv_h, uk_h, uv_h,
    out_ref,
    w_qkv, w_o, w_g, w_u, w_d, emb, ck, cv, uk, uv,
    pick, qs, ks, vs, rows_f,
    s1, r1, b2, s3, r3, b4, b5, b6, bm, b7, s8, r8, s9, r9, act, b12, b13, b14, s16, r16, s15, r15,
    load_sem, send_sem, recv_sem,
):
    g = lax.axis_index("guide")
    kv = lax.axis_index("kv")
    s = lax.axis_index("seq")
    z = lax.div(s, 4)
    x = lax.rem(s, 4)
    me = g * NS + s

    loads = [
        pltpu.make_async_copy(src, dst, load_sem.at[i])
        for i, (src, dst) in enumerate(
            [
                (qw_h, w_qkv.at[:, pl.ds(0, 1024)]),
                (kw_h, w_qkv.at[:, pl.ds(1024, 512)]),
                (vw_h, w_qkv.at[:, pl.ds(1536, 512)]),
                (ck_h, ck),
                (uk_h, uk),
                (cv_h, cv),
                (uv_h, uv),
                (ow_h, w_o),
                (gw_h, w_g),
                (uw_h, w_u),
                (dw_h, w_d),
                (emb_h, emb),
            ]
        )
    ]
    for load in loads:
        load.start()

    def peer(off):
        g2 = lax.rem(g + lax.div(off, 16), 2)
        z2 = lax.rem(z + lax.div(lax.rem(off, 16), 4), 4)
        x2 = lax.rem(x + lax.rem(off, 4), 4)
        return g2, z2 * 4 + x2

    def to_plane(body, count=NP):
        def one(off, carry):
            g2, s2 = peer(off)
            body(g2, s2)
            return carry

        lax.fori_loop(1, count, one, 0)

    def to_kv(body):
        for off in range(1, NKV):
            body(lax.rem(kv + off, NKV))

    def send(src, dst, i, device):
        pltpu.make_async_remote_copy(
            src_ref=src, dst_ref=dst, send_sem=send_sem.at[i], recv_sem=recv_sem.at[i],
            device_id=device, device_id_type=MESH,
        ).start()

    def whole(ref, i):
        return pltpu.make_async_remote_copy(
            src_ref=ref, dst_ref=ref, send_sem=send_sem.at[i], recv_sem=recv_sem.at[i],
            device_id={"guide": lax.rem(g + 1, 2)}, device_id_type=MESH,
        )

    barrier = pltpu.get_barrier_semaphore()
    to_plane(lambda g2, s2: pl.semaphore_signal(
        barrier, inc=1, device_id={"guide": g2, "seq": s2}, device_id_type=MESH))
    to_kv(lambda k2: pl.semaphore_signal(barrier, inc=1, device_id={"kv": k2}, device_id_type=MESH))

    x_in = hidden[...].astype(F32).reshape(16, WL)
    gain = gains[...]
    normed = (x_in * gain[0:1, :]).astype(BF16)
    x_sq = column_to_row(jnp.sum(x_in * x_in, axis=-1, keepdims=True))
    for i in range(3):
        loads[i].wait()
    part = nn_dot(normed, w_qkv[...])
    for j in range(NS):
        for k in range(NG):
            s1[k * NS + j, 0:8, :] = part[k * 8:(k + 1) * 8, j * 128:(j + 1) * 128]
            s1[k * NS + j, 8:9, :] = x_sq
    r1[me] = s1[me]
    pl.semaphore_wait(barrier, NP - 1 + NKV - 1)
    to_plane(lambda g2, s2: send(
        s1.at[g2 * NS + s2], r1.at[me], 0, {"guide": g2, "seq": s2}))

    first_row = (kv * NS + s) * ROWS

    def pick_rows(i, carry):
        base = pl.multiple_of(i * 256, 256)
        v = iota((256, 128), 0) + (first_row + base)
        for c in range(PICK // 128):
            pick[pl.ds(base, 256), c * 128:(c + 1) * 128] = one_hot(v == ids[c:c + 1, :])
        return carry

    lax.fori_loop(0, ROWS // 256, pick_rows, 0)

    whole(r1.at[pl.ds(0, NP - 1)], 0).wait_recv()
    total = jnp.sum(r1[...], axis=0)
    scale = lax.rsqrt(row_to_column(total[8:9, :], 8, 8 * g) / D + EPS)
    y = total[0:8, :] * scale
    turned = y * cosine[g] + pltpu.roll(y, 64, 1) * sine[g]
    y = jnp.where(s < 12, turned, y)
    y = jnp.where(s < 8, y * (D // H) ** (-0.5), y)
    b2[me] = y.astype(BF16).astype(F32)
    to_plane(lambda g2, s2: send(b2.at[me], b2.at[me], 1, {"guide": g2, "seq": s2}))

    picks = []
    r_ = iota((64, 128), 0)
    c_ = iota((64, 128), 1)
    for k in range(NG):
        held = jnp.zeros((64, 128), jnp.int32)
        for j in range(8):
            held = jnp.where(lax.div(r_, 8) == j, owner[k, j], held)
        same = lax.rem(c_, 8) == held
        head = lax.rem(r_, 8)
        blk = lax.div(c_, 8)
        picks.append((
            one_hot(same & (blk == head)),
            one_hot(same & (blk == 8 + lax.div(head, 2))),
            one_hot(same & (blk == 12 + lax.div(head, 2))),
        ))
    block = me
    limits = []
    for k, span in ((0, 256), (1, 64)):
        limit = jnp.zeros((64, span), jnp.int32)
        row = lax.div(iota((64, span), 0), 8)
        for j in range(8):
            limit = jnp.where(row == j, lengths[k, owner[k, j]], limit)
        limits.append(iota((64, span), 1) + block * span < limit)

    for i in range(3, 7):
        loads[i].wait()
    whole(b2.at[pl.ds(0, NP - 1)], 1).wait_recv()
    gathered = b2[...].reshape(NG, 128, 128).astype(BF16)
    lane_head = lax.div(lax.rem(iota((64, 128), 0), 8), 2)
    for k, span, keys, values in ((0, 256, ck, cv), (1, 64, uk, uv)):
        q = nn_dot(picks[k][0], gathered[k])
        for j in range(8):
            qs[k * 8 + j] = q[j * 8:(j + 1) * 8, :]
        wide = [jnp.where(lane_head == b, q, 0.0) for b in range(4)]
        scores = []
        for j in range(8):
            qj = jnp.concatenate([w[j * 8:(j + 1) * 8, :] for w in wide], axis=1).astype(BF16)
            scores.append(nt_dot(qj, keys[j]))
        score = jnp.concatenate(scores, axis=0)
        prob = jnp.where(limits[k], jnp.exp(ATTN_CAP * jnp.tanh(score / ATTN_CAP)), 0.0)
        denom = jnp.sum(prob, axis=1, keepdims=True)
        for j in range(8):
            pj = prob[j * 8:(j + 1) * 8, :].astype(BF16)
            full = nn_dot(pj, values[j])
            mine = jnp.zeros((8, 128), F32)
            for b in range(4):
                mine = jnp.where(lane_head[0:8, :] == b, full[:, b * 128:(b + 1) * 128], mine)
            s3[k * 8 + j, 0:8, :] = mine
            s3[k * 8 + j, 8:9, :] = column_to_row(denom[j * 8:(j + 1) * 8, :])

    tile_guide = lax.rem(s, 2)
    holds_tile = g == tile_guide

    def send_tile(off, carry):
        i = lax.rem(s + off, NS)
        send(s3.at[i], r3.at[me], 2, {"guide": lax.rem(i, 2), "seq": i})
        return carry

    lax.fori_loop(1, NS, send_tile, 0)

    @pl.when(jnp.logical_not(holds_tile))
    def _():
        send(s3.at[s], r3.at[me], 2, {"guide": tile_guide, "seq": s})

    for k in range(NG):
        kx = nn_dot(picks[k][1], gathered[k])
        vx = nn_dot(picks[k][2], gathered[k])
        for j in range(8):
            ks[k * 8 + j] = kx[j * 8:(j + 1) * 8, :]
            vs[k * 8 + j] = vx[j * 8:(j + 1) * 8, :]

    @pl.when(holds_tile)
    def _():
        r3[me] = s3[s]
        own = jnp.exp(ATTN_CAP * jnp.tanh(jnp.sum(qs[s] * ks[s], axis=1, keepdims=True) / ATTN_CAP))
        whole(r3.at[pl.ds(0, NP - 1)], 2).wait_recv()
        sums = jnp.sum(r3[...], axis=0)
        numer = sums[0:8, :] + own.astype(BF16).astype(F32) * vs[s]
        den = row_to_column(sums[8:9, :], 8) + own
        b4[s] = (numer / den).astype(BF16).astype(F32)
        to_plane(lambda g2, s2: send(b4.at[s], b4.at[s], 3, {"guide": g2, "seq": s2}))

    r_ = iota((128, 128), 0)
    c_ = iota((128, 128), 1)
    held = jnp.zeros((128, 128), jnp.int32)
    for i in range(16):
        held = jnp.where(lax.div(c_, 8) == i, owner[i // 8, i % 8], held)
    back = one_hot(
        (lax.div(r_, 16) == lax.rem(c_, 8))
        & (lax.rem(lax.div(r_, 8), 2) == lax.div(c_, 64))
        & (lax.rem(r_, 8) == held)
    )
    loads[7].wait()

    @pl.when(holds_tile)
    def _():
        whole(b4.at[pl.ds(0, NS - 1)], 3).wait_recv()

    @pl.when(jnp.logical_not(holds_tile))
    def _():
        whole(b4, 3).wait_recv()

    att = nn_dot(back, b4[...].reshape(128, 128).astype(BF16))
    att = jnp.concatenate([att[h * 16:(h + 1) * 16, :] for h in range(8)], axis=1).astype(BF16)
    b5[kv] = nn_dot(att, w_o[...])
    to_kv(lambda k2: send(b5.at[kv], b5.at[kv], 4, {"kv": k2}))
    whole(b5.at[pl.ds(0, NKV - 1)], 4).wait_recv()
    projected = (b5[0] + b5[1]) + (b5[2] + b5[3])
    b6[me] = column_to_row(jnp.sum(projected * projected, axis=-1, keepdims=True))
    to_plane(lambda g2, s2: send(b6.at[me], b6.at[me], 5, {"guide": g2, "seq": s2}))
    whole(b6.at[pl.ds(0, NP - 1)], 5).wait_recv()
    branch_sq = row_to_column(jnp.sum(b6[...], axis=0), 16)
    out_scale = lax.rsqrt(branch_sq / D + EPS)
    middle = x_in + projected * out_scale * gain[1:2, :]
    b7[me] = column_to_row(jnp.sum(middle * middle, axis=-1, keepdims=True))
    ffw_in = (middle * gain[2:3, :]).astype(BF16)

    loads[8].wait()
    loads[9].wait()

    def tile(g2, s2):
        r = g2 * NS + s2
        cols = pl.ds(pl.multiple_of(r * FB, FB), FB)
        s8[r, :, 0:FB] = nn_dot(ffw_in, w_g[:, cols]).astype(BF16)
        s8[r, :, FB:2 * FB] = nn_dot(ffw_in, w_u[:, cols]).astype(BF16)

    def tile_out(g2, s2):
        tile(g2, s2)
        send(s8.at[g2 * NS + s2], r8.at[me], 6, {"guide": g2, "seq": s2})

    tail = NP * FB
    g_tail = nn_dot(ffw_in, w_g[:, tail:FFL]).astype(BF16)
    u_tail = nn_dot(ffw_in, w_u[:, tail:FFL]).astype(BF16)
    for e in range(EXTRA):
        s9[e, :, 0:128] = g_tail[:, e * 128:(e + 1) * 128]
        s9[e, :, 128:256] = u_tail[:, e * 128:(e + 1) * 128]
    holds_extra = (g == 0) & (lax.rem(x, 2) == lax.rem(z, 2))
    extra = 2 * z + lax.div(x, 2)

    def send_extra(e, carry):
        z2 = lax.div(e, 2)
        s2 = 4 * z2 + 2 * lax.rem(e, 2) + lax.rem(z2, 2)

        @pl.when(jnp.logical_or(g != 0, s2 != s))
        def _():
            send(s9.at[e], r9.at[me], 7, {"guide": 0, "seq": s2})

        return carry

    lax.fori_loop(0, EXTRA, send_extra, 0)
    to_plane(tile_out)
    tile(g, s)
    r8[me] = s8[me]
    to_plane(lambda g2, s2: send(b7.at[me], b7.at[me], 8, {"guide": g2, "seq": s2}))
    bm[s, 0:16, :] = middle
    bm[s, 16:18, :] = gain[3:5, :]
    to_plane(lambda g2, s2: send(bm.at[s], bm.at[s], 9, {"seq": s2}), NS)

    whole(b7.at[pl.ds(0, NP - 1)], 8).wait_recv()
    ffw_scale = lax.rsqrt(row_to_column(jnp.sum(b7[...], axis=0), 16) / D + EPS)

    def activate(gate, up):
        gate = gate * ffw_scale
        return (jax.nn.gelu(gate, approximate=True) * (up * ffw_scale)).astype(BF16)

    whole(r8.at[pl.ds(0, NP - 1)], 6).wait_recv()
    sums = jnp.sum(r8[...].astype(F32), axis=0)
    mine = pl.ds(pl.multiple_of(me * FB, FB), FB)
    act[:, mine] = activate(sums[:, 0:FB], sums[:, FB:2 * FB])
    to_plane(lambda g2, s2: send(act.at[:, mine], act.at[:, mine], 10, {"guide": g2, "seq": s2}))

    @pl.when(holds_extra)
    def _():
        r9[me] = s9[extra]
        whole(r9.at[pl.ds(0, NP - 1)], 7).wait_recv()
        sums = jnp.sum(r9[...].astype(F32), axis=0)
        cols = pl.ds(pl.multiple_of(tail + extra * 128, 128), 128)
        act[:, cols] = activate(sums[:, 0:128], sums[:, 128:256])
        to_plane(lambda g2, s2: send(act.at[:, cols], act.at[:, cols], 11, {"guide": g2, "seq": s2}))

    loads[10].wait()
    whole(act.at[:, pl.ds(0, (NP - 1) * FB)], 10).wait_recv()

    @pl.when(holds_extra)
    def _():
        whole(act.at[:, pl.ds(0, (EXTRA - 1) * 128)], 11).wait_recv()

    @pl.when(jnp.logical_not(holds_extra))
    def _():
        whole(act.at[:, pl.ds(0, EXTRA * 128)], 11).wait_recv()

    b12[kv] = nn_dot(act[...], w_d[...])
    to_kv(lambda k2: send(b12.at[kv], b12.at[kv], 12, {"kv": k2}))
    whole(b12.at[pl.ds(0, NKV - 1)], 12).wait_recv()
    ffw_out = (b12[0] + b12[1]) + (b12[2] + b12[3])
    b14[s] = ffw_out
    b13[me] = column_to_row(jnp.sum(ffw_out * ffw_out, axis=-1, keepdims=True))
    to_plane(lambda g2, s2: send(b14.at[s], b14.at[s], 14, {"seq": s2}), NS)
    to_plane(lambda g2, s2: send(b13.at[me], b13.at[me], 13, {"guide": g2, "seq": s2}))

    loads[11].wait()
    whole(bm.at[pl.ds(0, NS - 1)], 9).wait_recv()
    whole(b13.at[pl.ds(0, NP - 1)], 13).wait_recv()
    branch_scale = lax.rsqrt(row_to_column(jnp.sum(b13[...], axis=0), 16) / D + EPS)
    whole(b14.at[pl.ds(0, NS - 1)], 14).wait_recv()
    last_sq = jnp.zeros((16, 1), F32)
    for t in range(NS):
        last = bm[t, 0:16, :] + b14[t] * branch_scale * bm[t, 16:17, :]
        last_sq = last_sq + jnp.sum(last * last, axis=-1, keepdims=True)
        rows_f[:, t * WL:(t + 1) * WL] = last * bm[t, 17:18, :]
    s15[...] = column_to_row(last_sq)
    other = {"guide": lax.rem(g + 1, 2)}
    send(s15, r15, 15, other)

    full = nt_dot(rows_f[...].astype(BF16), emb[...])
    high = full.astype(BF16)
    low = (full - high.astype(F32)).astype(BF16)
    logit = nn_dot(jnp.concatenate([high, low], axis=0), pick[...])
    logit = logit[0:16, :] + logit[16:32, :]
    lower = jnp.concatenate([logit[0:4, :], logit[8:12, :]], axis=0)
    upper = jnp.concatenate([logit[4:8, :], logit[12:16, :]], axis=0)
    s16[...] = jnp.where(g == 0, upper, lower)
    send(s16, r16, 16, other)
    keep = jnp.where(g == 0, lower, upper)
    whole(r15, 15).wait_recv()
    lanes = iota((8, 128), 1)
    rowi = iota((8, 128), 0)
    want = lax.div(rowi, 4) * 8 + 4 * g + lax.rem(rowi, 4)
    sq = jnp.sum(jnp.where(lanes == want, jnp.broadcast_to(s15[...] + r15[...], (8, 128)), 0.0),
                 axis=1, keepdims=True)
    final_scale = lax.rsqrt(sq / D + EPS)
    share = jnp.zeros((4, 1), F32)
    for i in range(4):
        share = jnp.where(iota((4, 1), 0) == i, guidance[4 * g + i], share)
    whole(r16, 16).wait_recv()
    capped = LOGIT_CAP * jnp.tanh((keep + r16[...]) * final_scale / LOGIT_CAP)
    out_ref[...] = capped[4:8, :] + share * (capped[0:4, :] - capped[4:8, :])

    whole(s1.at[pl.ds(0, NP - 1)], 0).wait_send()
    whole(b2.at[pl.ds(0, NP - 1)], 1).wait_send()

    @pl.when(holds_tile)
    def _():
        whole(s3.at[pl.ds(0, NS - 1)], 2).wait_send()
        for_out = s1.at[pl.ds(0, NP - 1), pl.ds(0, 8)]
        whole(for_out, 3).wait_send()

    @pl.when(jnp.logical_not(holds_tile))
    def _():
        whole(s3, 2).wait_send()

    whole(b5.at[pl.ds(0, NKV - 1)], 4).wait_send()
    whole(b6.at[pl.ds(0, NP - 1)], 5).wait_send()
    whole(s8.at[pl.ds(0, NP - 1)], 6).wait_send()

    @pl.when(holds_extra)
    def _():
        whole(s9.at[pl.ds(0, EXTRA - 1)], 7).wait_send()
        whole(act.at[:, pl.ds(0, (NP - 1) * 128)], 11).wait_send()

    @pl.when(jnp.logical_not(holds_extra))
    def _():
        whole(s9, 7).wait_send()

    whole(b7.at[pl.ds(0, NP - 1)], 8).wait_send()
    whole(bm.at[pl.ds(0, NS - 1)], 9).wait_send()
    whole(act.at[:, pl.ds(0, (NP - 1) * FB)], 10).wait_send()
    whole(b12.at[pl.ds(0, NKV - 1)], 12).wait_send()
    whole(b13.at[pl.ds(0, NP - 1)], 13).wait_send()
    whole(b14.at[pl.ds(0, NS - 1)], 14).wait_send()
    whole(s15, 15).wait_send()
    whole(s16, 16).wait_send()


def on_device(
    hidden, lengths, slot_owner, allowed_ids, guidance,
    pre_attn_gain, post_attn_gain, pre_ffw_gain, post_ffw_gain, final_gain,
    query_weight, key_weight, value_weight, output_weight,
    gate_weight, up_weight, down_weight, embedding,
    cond_keys, cond_values, uncond_keys, uncond_values,
):
    position = lengths.astype(F32)
    frequency = THETA ** (-2.0 * jnp.arange(HD // 2, dtype=F32) / HD)
    angles = position[:, :, None] * frequency
    cosine = jnp.cos(angles)
    sine = jnp.sin(angles)
    cosine = jnp.concatenate([cosine, cosine], axis=-1)
    sine = jnp.concatenate([-sine, sine], axis=-1)
    gains = jnp.stack([pre_attn_gain, post_attn_gain, pre_ffw_gain, post_ffw_gain, final_gain])
    smem = pl.BlockSpec(memory_space=pltpu.SMEM)
    vmem = pl.BlockSpec(memory_space=pltpu.VMEM)
    hbm = pl.BlockSpec(memory_space=pl.ANY)
    return pl.pallas_call(
        step_kernel,
        out_shape=jax.ShapeDtypeStruct((4, PICK), F32),
        in_specs=[smem] * 3 + [vmem] * 5 + [hbm] * 12,
        out_specs=vmem,
        scratch_shapes=[
            pltpu.VMEM((WL, 2048), BF16),
            pltpu.VMEM((1024, WL), BF16),
            pltpu.VMEM((WL, FFL), BF16),
            pltpu.VMEM((WL, FFL), BF16),
            pltpu.VMEM((FFL, WL), BF16),
            pltpu.VMEM((ROWS, HALF), BF16),
            pltpu.VMEM((8, 256, 512), BF16),
            pltpu.VMEM((8, 256, 512), BF16),
            pltpu.VMEM((8, 64, 512), BF16),
            pltpu.VMEM((8, 64, 512), BF16),
            pltpu.VMEM((ROWS, PICK), BF16),
            pltpu.VMEM((16, 8, 128), F32),
            pltpu.VMEM((16, 8, 128), F32),
            pltpu.VMEM((16, 8, 128), F32),
            pltpu.VMEM((16, HALF), F32),
            pltpu.VMEM((NP, 9, 128), F32),
            pltpu.VMEM((NP, 9, 128), F32),
            pltpu.VMEM((NP, 8, 128), F32),
            pltpu.VMEM((16, 9, 128), F32),
            pltpu.VMEM((NP, 9, 128), F32),
            pltpu.VMEM((16, 8, 128), F32),
            pltpu.VMEM((NKV, 16, WL), F32),
            pltpu.VMEM((NP, 1, 128), F32),
            pltpu.VMEM((NS, 18, WL), F32),
            pltpu.VMEM((NP, 1, 128), F32),
            pltpu.VMEM((NP, 16, 2 * FB), BF16),
            pltpu.VMEM((NP, 16, 2 * FB), BF16),
            pltpu.VMEM((EXTRA, 16, 256), BF16),
            pltpu.VMEM((NP, 16, 256), BF16),
            pltpu.VMEM((16, FFL), BF16),
            pltpu.VMEM((NKV, 16, WL), F32),
            pltpu.VMEM((NP, 1, 128), F32),
            pltpu.VMEM((NS, 16, WL), F32),
            pltpu.VMEM((8, PICK), F32),
            pltpu.VMEM((8, PICK), F32),
            pltpu.VMEM((1, 128), F32),
            pltpu.VMEM((1, 128), F32),
            pltpu.SemaphoreType.DMA((12,)),
            pltpu.SemaphoreType.DMA((17,)),
            pltpu.SemaphoreType.DMA((17,)),
        ],
        compiler_params=pltpu.CompilerParams(
            collective_id=0, has_side_effects=True, vmem_limit_bytes=60 * 1024 * 1024
        ),
        name="decode_step",
    )(
        lengths, slot_owner, guidance, hidden, allowed_ids.reshape(8, 128), cosine, sine, gains,
        query_weight, key_weight, value_weight, output_weight, gate_weight, up_weight, down_weight,
        embedding, cond_keys, cond_values, uncond_keys, uncond_values,
    )


def solution(mesh):
    return jax.shard_map(
        on_device,
        mesh=mesh,
        in_specs=(
            P(None, None, ("guide", "seq")),
            P(),
            P(),
            P(("kv", "seq")),
            P(),
            P(("guide", "seq")),
            P(("guide", "seq")),
            P(("guide", "seq")),
            P(("guide", "seq")),
            P(("guide", "seq")),
            P(("guide", "seq"), "kv"),
            P(("guide", "seq"), "kv"),
            P(("guide", "seq"), "kv"),
            P("kv", ("guide", "seq")),
            P(("guide", "seq"), "kv"),
            P(("guide", "seq"), "kv"),
            P("kv", ("guide", "seq")),
            P(("kv", "seq"), "guide"),
            P(None, ("guide", "seq"), "kv"),
            P(None, ("guide", "seq"), "kv"),
            P(None, ("guide", "seq"), "kv"),
            P(None, ("guide", "seq"), "kv"),
        ),
        out_specs=P("guide", ("kv", "seq")),
        check_vma=False,
    )
```

time: 686 us -> 88.1 us (0.13)
  blocking collectives: 383 us -> 0 us
  waiting for transfers between devices: 233 us -> 0 us
  Pallas kernels: 0 us -> 75.8 us
  matrix products: 25 us -> 0 us
  between operations: 15.4 us -> 0.02 us
  other arithmetic: 10.9 us -> 1.49 us
  local copies, waits for them, and re-layouts: 17.3 us -> 10.4 us
    psum x7 -> x0, blocking collectives: 365 us -> none  [the longest x1 70 us: on_device(): lax.psum((square_part, query_part, key_part, value_part), ('guide', 'seq'))]
    psum x4 -> x0, waiting for transfers between devices: 233 us -> none  [the longest x2 189 us: on_device(): numer_sum, denom_sum = lax.psum((numer_part, denom_part), ('guide', 'seq'))]
    pallas_call x0 -> x1, Pallas kernels: none -> 75.8 us  [on_device(): pl.pallas_call(step_kernel, out_shape=jax.ShapeDtypeStruct((4, PICK), F32...]
    dot_general x17 -> x0, matrix products: 25 us -> none  [the longest x1 4.75 us: on_device(): jnp.einsum('sd,ad->sa', half_rows.reshape(stream_count, half_rows.shape[2...]
    all_gather x1 -> x0, blocking collectives: 18.4 us -> none  [on_device(): half_rows = lax.all_gather(final_rows, 'seq', axis=2, tiled=True)]
    gather x1 -> x0, local copies, waits for them, and re-layouts: 14.8 us -> none  [on_device(): picked = jnp.take(embedding, allowed_ids - block_first, axis=0)]
    unnamed x26 -> x3, local copies, waits for them, and re-layouts: 1.16 us -> 9.09 us
  transfers between devices with their start and end apart: 5 -> 0, of which waited for: 4 -> 0; matrix products, arithmetic and copies ran while one was open for 4% -> 0% of each run, Pallas kernels for 0% -> 0%
where the time goes in v1:
time: 88.1 us; the launch traced here: 87.7 us
  Pallas kernels  75.8 us (86%)
  local copies, waits for them, and re-layouts  10.4 us (12%)
  other arithmetic  1.49 us (2%)
    pallas_call x1, Pallas kernels, on_device(): pl.pallas_call(step_kernel, out_shape=jax.ShapeDtypeStruct((4, PICK), F32...  75.8 us
    unnamed x3, local copies, waits for them, and re-layouts  9.09 us

profile of v1, /device:TPU:1, one launch (start us, length us, event | category | flops | bytes accessed | tf_op | source)
XLA Modules:
  0.0 87.7 jit_solution(14814740105954341708)
XLA Ops:
  0.0 0.7 convert_element_type.3
  0.7 1.3 %stack.23.gains = f32[5,144]{1,0:T(8,128)} concatenate(f32[1,144]{1,0:T(1,128)} %bitcast.7, f32[1,144]{1,0:T(1,128)} %bitcast.8, f32[1,144]{1,0:T(1,128)} %bitcast.9, f32[1,144]{1,0:T(1,128)} %bitcast.10, f32[1,144]{1,0:T(1,128)} %bitcast.11), dimensions={0} | concatenate | bytes 5760 | tf_op jit(solution)/shard_map/stack | solution.py:455
  2.0 0.1 fusion
  2.2 0.7 pad_maximum_fusion
  2.8 2.0 %copy.23.ow_h = bf16[1024,144]{1,0:T(8,128)(2,1)} copy(bf16[1024,144]{0,1:T(8,128)(2,1)} %param.35) | data formatting | bytes 589824 | tf_op args[13]
  4.8 5.8 %copy.24.dw_h = bf16[9216,144]{1,0:T(8,128)(2,1)} copy(bf16[9216,144]{0,1:T(8,128)(2,1)} %param.38) | data formatting | bytes 5308416 | tf_op args[16]
  10.6 75.8 %decode_step.1 = f32[4,1024]{1,0:T(4,128)} custom-call(s32[2,8]{1,0:T(2,128)} %lengths.1, s32[2,8]{1,0:T(2,128)} %owner.1, f32[8]{0:T(128)} %guidance.1, bf16[2,8,144]{2,1,0:T(8,128)(2,1)} %hidden.1, s32[8,128]{1,0:T(8,128)} %bitcast.6, f32[2,8,128]{2,1,0:T(8,128)} %get-tuple-element.8.cosine, f32[2,8,128]{2,1,0:T(8,128)} %get-tuple-element.9.sine, ...), custom_call_target="tpu_custom_call" | custom-call | tf_op jit(solution)/shard_map/decode_step/pallas_call | solution.py:459
  86.4 1.3 %copy.26 = f32[4,1024]{1,0:T(4,128)} copy(f32[4,1024]{1,0:T(4,128)} %decode_step.1) | data formatting | bytes 32768
  (1 shorter events, 0.0 us)

commit v2 on v1

--- a/solution.py
+++ b/solution.py
@@ -1,5 +1,8 @@
+import functools
+
 import jax
 import jax.numpy as jnp
+import numpy as np
 from jax import lax
 from jax.experimental import pallas as pl
 from jax.experimental.pallas import tpu as pltpu
@@ -55,12 +58,13 @@
 
 
 def step_kernel(
-    lengths, owner, guidance, hidden, ids, cosine, sine, gains,
+    lengths, owner, guidance, hidden, ids, freq, gain0, gain1, gain2, gain3, gain4,
     qw_h, kw_h, vw_h, ow_h, gw_h, uw_h, dw_h, emb_h, ck_h, cv_h, uk_h, uv_h,
-    out_ref,
+    base_ref, lift_ref,
     w_qkv, w_o, w_g, w_u, w_d, emb, ck, cv, uk, uv,
-    pick, qs, ks, vs, rows_f,
-    s1, r1, b2, s3, r3, b4, b5, b6, bm, b7, s8, r8, s9, r9, act, b12, b13, b14, s16, r16, s15, r15,
+    pick, table, qs, ks, vs, rows_f,
+    s1, r1, b2, s3, r3, b4, b5, b6, bm, act, b12, b13, b14, s16, r16, s15, r15,
+    pa, qa, ka, sa, ra, ta, ua, va, wa, xa, pb, qb, kb, sb, rb, tb, ub, vb, wb, xb,
     load_sem, send_sem, recv_sem,
 ):
     g = lax.axis_index("guide")
@@ -89,7 +93,7 @@
             ]
         )
     ]
-    for load in loads:
+    for load in loads[0:3]:
         load.start()
 
     def peer(off):
@@ -122,26 +126,93 @@
             device_id={"guide": lax.rem(g + 1, 2)}, device_id_type=MESH,
         )
 
+    pending = []
+
+    def finish():
+        for ref, i, when in pending:
+            if when is None:
+                whole(ref, i).wait_send()
+            else:
+                pl.when(when)(functools.partial(lambda ref, i: whole(ref, i).wait_send(), ref, i))
+
     barrier = pltpu.get_barrier_semaphore()
     to_plane(lambda g2, s2: pl.semaphore_signal(
         barrier, inc=1, device_id={"guide": g2, "seq": s2}, device_id_type=MESH))
     to_kv(lambda k2: pl.semaphore_signal(barrier, inc=1, device_id={"kv": k2}, device_id_type=MESH))
 
+    other = {"guide": lax.rem(g + 1, 2)}
+    tail = NP * FB
+    holds_extra = (lax.rem(x, 2) == lax.rem(z, 2)) & (lax.div(z, 2) == g)
+    extra = 2 * z + lax.div(x, 2)
+    set_a = (pa, qa, ka, sa, ra, ta, ua, va, wa, xa)
+    set_b = (pb, qb, kb, sb, rb, tb, ub, vb, wb, xb)
+
+    def ffw_product(rows, buffers, base):
+        away, _, keep, _, _, tail_away, _, tail_keep, _, _ = buffers
+        high = rows.astype(BF16)
+        low = (rows - high.astype(F32)).astype(BF16)
+        both = jnp.concatenate([high, low], axis=0)
+
+        def product(weight, cols):
+            wide = nn_dot(both, weight[:, cols])
+            return wide[0:16, :] + wide[16:32, :]
+
+        for whose, main, rest in ((1 - g, away, tail_away), (g, keep, tail_keep)):
+            cols = pl.ds(pl.multiple_of(whose * (NS * FB), NS * FB), NS * FB)
+            tail_cols = pl.ds(pl.multiple_of(tail + whose * 512, 512), 512)
+            for at, weight in ((0, w_g), (1, w_u)):
+                part = product(weight, cols).astype(main.dtype)
+                for c in range(NS):
+                    main[c, :, at * FB:(at + 1) * FB] = part[:, c * FB:(c + 1) * FB]
+                part = product(weight, tail_cols).astype(rest.dtype)
+                for c in range(4):
+                    rest[c, :, at * 128:(at + 1) * 128] = part[:, c * 128:(c + 1) * 128]
+            if main is away:
+                send(away, buffers[1], base, other)
+                send(tail_away, buffers[6], base + 1, other)
+                pending.append((away, base, None))
+                pending.append((tail_away, base + 1, None))
+
+    def ffw_combine(buffers, base):
+        _, came, keep, out, _, _, tail_came, tail_keep, tail_out, _ = buffers
+        whole(came, base).wait_recv()
+        whole(tail_came, base + 1).wait_recv()
+        out[...] = (keep[...] + came[...].astype(F32)).astype(BF16)
+        tail_out[...] = (tail_keep[...] + tail_came[...].astype(F32)).astype(BF16)
+
+    def ffw_send(buffers, base):
+        _, _, _, out, into, _, _, _, tail_out, tail_into = buffers
+
+        def one(q, carry):
+            z2 = 2 * g + lax.div(q, 2)
+            s2 = 4 * z2 + 2 * lax.rem(q, 2) + lax.rem(z2, 2)
+
+            @pl.when(s2 != s)
+            def _():
+                send(tail_out.at[q], tail_into.at[s], base + 1, {"seq": s2})
+
+            return carry
+
+        lax.fori_loop(0, 4, one, 0)
+        to_plane(lambda g2, s2: send(out.at[s2], into.at[s], base, {"seq": s2}), NS)
+        into[s] = out[s]
+        pending.append((out.at[pl.ds(0, NS - 1)], base, None))
+        pending.append((tail_out.at[pl.ds(0, 3)], base + 1, holds_extra))
+        pending.append((tail_out, base + 1, jnp.logical_not(holds_extra)))
+
     x_in = hidden[...].astype(F32).reshape(16, WL)
-    gain = gains[...]
-    normed = (x_in * gain[0:1, :]).astype(BF16)
+    normed = (x_in * gain0[...]).astype(BF16)
     x_sq = column_to_row(jnp.sum(x_in * x_in, axis=-1, keepdims=True))
     for i in range(3):
         loads[i].wait()
+    for load in loads[3:12]:
+        load.start()
     part = nn_dot(normed, w_qkv[...])
     for j in range(NS):
         for k in range(NG):
             s1[k * NS + j, 0:8, :] = part[k * 8:(k + 1) * 8, j * 128:(j + 1) * 128]
             s1[k * NS + j, 8:9, :] = x_sq
     r1[me] = s1[me]
-    pl.semaphore_wait(barrier, NP - 1 + NKV - 1)
-    to_plane(lambda g2, s2: send(
-        s1.at[g2 * NS + s2], r1.at[me], 0, {"guide": g2, "seq": s2}))
 
     first_row = (kv * NS + s) * ROWS
 
@@ -152,17 +223,40 @@
             pick[pl.ds(base, 256), c * 128:(c + 1) * 128] = one_hot(v == ids[c:c + 1, :])
         return carry
 
+    def pick_table(first, count):
+        def one(i, carry):
+            cols = pl.ds(pl.multiple_of(i * 256, 256), 256)
+            table[cols, :] = lax.dot_general(
+                emb[:, cols], pick[...], (((0,), (0,)), ((), ())), preferred_element_type=F32
+            ).astype(BF16)
+            return carry
+
+        lax.fori_loop(first, first + count, one, 0)
+
+    turn_row = iota((8, 128), 0)
+    position = jnp.zeros((8, 128), F32)
+    for i in range(8):
+        position = jnp.where(turn_row == i, lengths[g, i].astype(F32), position)
+    angle = position * freq[...]
+    cosine = jnp.cos(angle)
+    sine = jnp.sin(angle)
+    sine = jnp.where(iota((8, 128), 1) < 64, -sine, sine)
+    pl.semaphore_wait(barrier, NP - 1 + NKV - 1)
+    to_plane(lambda g2, s2: send(
+        s1.at[g2 * NS + s2], r1.at[me], 0, {"guide": g2, "seq": s2}))
+    pending.append((s1.at[pl.ds(0, NP - 1)], 0, None))
+
     lax.fori_loop(0, ROWS // 256, pick_rows, 0)
-
     whole(r1.at[pl.ds(0, NP - 1)], 0).wait_recv()
     total = jnp.sum(r1[...], axis=0)
     scale = lax.rsqrt(row_to_column(total[8:9, :], 8, 8 * g) / D + EPS)
     y = total[0:8, :] * scale
-    turned = y * cosine[g] + pltpu.roll(y, 64, 1) * sine[g]
+    turned = y * cosine + pltpu.roll(y, 64, 1) * sine
     y = jnp.where(s < 12, turned, y)
     y = jnp.where(s < 8, y * (D // H) ** (-0.5), y)
     b2[me] = y.astype(BF16).astype(F32)
     to_plane(lambda g2, s2: send(b2.at[me], b2.at[me], 1, {"guide": g2, "seq": s2}))
+    pending.append((b2.at[pl.ds(0, NP - 1)], 1, None))
 
     picks = []
     r_ = iota((64, 128), 0)
@@ -188,6 +282,9 @@
             limit = jnp.where(row == j, lengths[k, owner[k, j]], limit)
         limits.append(iota((64, span), 1) + block * span < limit)
 
+    loads[8].wait()
+    loads[9].wait()
+    ffw_product(x_in * gain2[...], set_a, 6)
     for i in range(3, 7):
         loads[i].wait()
     whole(b2.at[pl.ds(0, NP - 1)], 1).wait_recv()
@@ -228,12 +325,20 @@
     def _():
         send(s3.at[s], r3.at[me], 2, {"guide": tile_guide, "seq": s})
 
+    pending.append((s3.at[pl.ds(0, NS - 1)], 2, holds_tile))
+    pending.append((s3, 2, jnp.logical_not(holds_tile)))
+    pending.append((s1.at[pl.ds(0, NP - 1), pl.ds(0, 8)], 3, holds_tile))
+
     for k in range(NG):
         kx = nn_dot(picks[k][1], gathered[k])
         vx = nn_dot(picks[k][2], gathered[k])
         for j in range(8):
             ks[k * 8 + j] = kx[j * 8:(j + 1) * 8, :]
             vs[k * 8 + j] = vx[j * 8:(j + 1) * 8, :]
+
+    ffw_combine(set_a, 6)
+    loads[11].wait()
+    pick_table(0, 1)
 
     @pl.when(holds_tile)
     def _():
@@ -256,6 +361,7 @@
         & (lax.rem(lax.div(r_, 8), 2) == lax.div(c_, 64))
         & (lax.rem(r_, 8) == held)
     )
+    pick_table(1, 2)
     loads[7].wait()
 
     @pl.when(holds_tile)
@@ -268,82 +374,66 @@
 
     att = nn_dot(back, b4[...].reshape(128, 128).astype(BF16))
     att = jnp.concatenate([att[h * 16:(h + 1) * 16, :] for h in range(8)], axis=1).astype(BF16)
-    b5[kv] = nn_dot(att, w_o[...])
+    b5[kv] = nt_dot(att, w_o[...])
     to_kv(lambda k2: send(b5.at[kv], b5.at[kv], 4, {"kv": k2}))
+    pending.append((b5.at[pl.ds(0, NKV - 1)], 4, None))
+    ffw_send(set_a, 17)
+    pick_table(3, 1)
     whole(b5.at[pl.ds(0, NKV - 1)], 4).wait_recv()
     projected = (b5[0] + b5[1]) + (b5[2] + b5[3])
-    b6[me] = column_to_row(jnp.sum(projected * projected, axis=-1, keepdims=True))
+    branch = projected * gain1[...]
+    b6[me, 0:1, :] = column_to_row(jnp.sum(projected * projected, axis=-1, keepdims=True))
+    b6[me, 1:2, :] = column_to_row(jnp.sum(x_in * branch, axis=-1, keepdims=True))
+    b6[me, 2:3, :] = column_to_row(jnp.sum(branch * branch, axis=-1, keepdims=True))
+    b6[me, 3:4, :] = x_sq
     to_plane(lambda g2, s2: send(b6.at[me], b6.at[me], 5, {"guide": g2, "seq": s2}))
+    pending.append((b6.at[pl.ds(0, NP - 1)], 5, None))
+    ffw_product(branch * gain2[...], set_b, 19)
+    ffw_combine(set_b, 19)
+    ffw_send(set_b, 21)
+    pick_table(4, 3)
     whole(b6.at[pl.ds(0, NP - 1)], 5).wait_recv()
-    branch_sq = row_to_column(jnp.sum(b6[...], axis=0), 16)
-    out_scale = lax.rsqrt(branch_sq / D + EPS)
-    middle = x_in + projected * out_scale * gain[1:2, :]
-    b7[me] = column_to_row(jnp.sum(middle * middle, axis=-1, keepdims=True))
-    ffw_in = (middle * gain[2:3, :]).astype(BF16)
-
-    loads[8].wait()
-    loads[9].wait()
-
-    def tile(g2, s2):
-        r = g2 * NS + s2
-        cols = pl.ds(pl.multiple_of(r * FB, FB), FB)
-        s8[r, :, 0:FB] = nn_dot(ffw_in, w_g[:, cols]).astype(BF16)
-        s8[r, :, FB:2 * FB] = nn_dot(ffw_in, w_u[:, cols]).astype(BF16)
-
-    def tile_out(g2, s2):
-        tile(g2, s2)
-        send(s8.at[g2 * NS + s2], r8.at[me], 6, {"guide": g2, "seq": s2})
-
-    tail = NP * FB
-    g_tail = nn_dot(ffw_in, w_g[:, tail:FFL]).astype(BF16)
-    u_tail = nn_dot(ffw_in, w_u[:, tail:FFL]).astype(BF16)
-    for e in range(EXTRA):
-        s9[e, :, 0:128] = g_tail[:, e * 128:(e + 1) * 128]
-        s9[e, :, 128:256] = u_tail[:, e * 128:(e + 1) * 128]
-    holds_extra = (g == 0) & (lax.rem(x, 2) == lax.rem(z, 2))
-    extra = 2 * z + lax.div(x, 2)
-
-    def send_extra(e, carry):
-        z2 = lax.div(e, 2)
-        s2 = 4 * z2 + 2 * lax.rem(e, 2) + lax.rem(z2, 2)
-
-        @pl.when(jnp.logical_or(g != 0, s2 != s))
-        def _():
-            send(s9.at[e], r9.at[me], 7, {"guide": 0, "seq": s2})
-
-        return carry
-
-    lax.fori_loop(0, EXTRA, send_extra, 0)
-    to_plane(tile_out)
-    tile(g, s)
-    r8[me] = s8[me]
-    to_plane(lambda g2, s2: send(b7.at[me], b7.at[me], 8, {"guide": g2, "seq": s2}))
-    bm[s, 0:16, :] = middle
-    bm[s, 16:18, :] = gain[3:5, :]
-    to_plane(lambda g2, s2: send(bm.at[s], bm.at[s], 9, {"seq": s2}), NS)
-
-    whole(b7.at[pl.ds(0, NP - 1)], 8).wait_recv()
-    ffw_scale = lax.rsqrt(row_to_column(jnp.sum(b7[...], axis=0), 16) / D + EPS)
-
-    def activate(gate, up):
-        gate = gate * ffw_scale
-        return (jax.nn.gelu(gate, approximate=True) * (up * ffw_scale)).astype(BF16)
-
-    whole(r8.at[pl.ds(0, NP - 1)], 6).wait_recv()
-    sums = jnp.sum(r8[...].astype(F32), axis=0)
+    sums = jnp.sum(b6[...], axis=0)
+    out_scale = lax.rsqrt(row_to_column(sums[0:1, :], 16) / D + EPS)
+    middle_sq = (
+        row_to_column(sums[3:4, :], 16)
+        + 2.0 * out_scale * row_to_column(sums[1:2, :], 16)
+        + out_scale * out_scale * row_to_column(sums[2:3, :], 16)
+    )
+    ffw_scale = lax.rsqrt(jnp.maximum(middle_sq, 0.0) / D + EPS)
+    bm[s, 0:16, :] = x_in + branch * out_scale
+    bm[s, 16:17, :] = gain3[...]
+    bm[s, 17:18, :] = gain4[...]
+
+    def activate(first, second):
+        n = first.shape[1] // 2
+        both = (first + out_scale * second) * ffw_scale
+        return (jax.nn.gelu(both[:, 0:n], approximate=True) * both[:, n:2 * n]).astype(BF16)
+
+    def gathered_sum(ref):
+        return jnp.sum(ref[...].astype(F32), axis=0)
+
+    whole(ra.at[pl.ds(0, NS - 1)], 17).wait_recv()
+    first = gathered_sum(ra)
+    whole(rb.at[pl.ds(0, NS - 1)], 21).wait_recv()
     mine = pl.ds(pl.multiple_of(me * FB, FB), FB)
-    act[:, mine] = activate(sums[:, 0:FB], sums[:, FB:2 * FB])
+    act[:, mine] = activate(first, gathered_sum(rb))
     to_plane(lambda g2, s2: send(act.at[:, mine], act.at[:, mine], 10, {"guide": g2, "seq": s2}))
+    pending.append((act.at[:, pl.ds(0, (NP - 1) * FB)], 10, None))
+    pending.append((act.at[:, pl.ds(0, (NP - 1) * 128)], 11, holds_extra))
 
     @pl.when(holds_extra)
     def _():
-        r9[me] = s9[extra]
-        whole(r9.at[pl.ds(0, NP - 1)], 7).wait_recv()
-        sums = jnp.sum(r9[...].astype(F32), axis=0)
+        own = extra - 4 * g
+        xa[s] = wa[own]
+        xb[s] = wb[own]
+        whole(xa.at[pl.ds(0, NS - 1)], 18).wait_recv()
+        whole(xb.at[pl.ds(0, NS - 1)], 22).wait_recv()
         cols = pl.ds(pl.multiple_of(tail + extra * 128, 128), 128)
-        act[:, cols] = activate(sums[:, 0:128], sums[:, 128:256])
+        act[:, cols] = activate(gathered_sum(xa), gathered_sum(xb))
         to_plane(lambda g2, s2: send(act.at[:, cols], act.at[:, cols], 11, {"guide": g2, "seq": s2}))
 
+    pick_table(7, 2)
     loads[10].wait()
     whole(act.at[:, pl.ds(0, (NP - 1) * FB)], 10).wait_recv()
 
@@ -355,38 +445,39 @@
     def _():
         whole(act.at[:, pl.ds(0, EXTRA * 128)], 11).wait_recv()
 
-    b12[kv] = nn_dot(act[...], w_d[...])
+    to_plane(lambda g2, s2: send(bm.at[s], bm.at[s], 9, {"seq": s2}), NS)
+    pending.append((bm.at[pl.ds(0, NS - 1)], 9, None))
+    b12[kv] = nt_dot(act[...], w_d[...])
     to_kv(lambda k2: send(b12.at[kv], b12.at[kv], 12, {"kv": k2}))
+    pending.append((b12.at[pl.ds(0, NKV - 1)], 12, None))
     whole(b12.at[pl.ds(0, NKV - 1)], 12).wait_recv()
     ffw_out = (b12[0] + b12[1]) + (b12[2] + b12[3])
-    b14[s] = ffw_out
+    b14[s] = ffw_out.astype(BF16)
     b13[me] = column_to_row(jnp.sum(ffw_out * ffw_out, axis=-1, keepdims=True))
     to_plane(lambda g2, s2: send(b14.at[s], b14.at[s], 14, {"seq": s2}), NS)
+    pending.append((b14.at[pl.ds(0, NS - 1)], 14, None))
     to_plane(lambda g2, s2: send(b13.at[me], b13.at[me], 13, {"guide": g2, "seq": s2}))
-
-    loads[11].wait()
+    pending.append((b13.at[pl.ds(0, NP - 1)], 13, None))
+
     whole(bm.at[pl.ds(0, NS - 1)], 9).wait_recv()
     whole(b13.at[pl.ds(0, NP - 1)], 13).wait_recv()
     branch_scale = lax.rsqrt(row_to_column(jnp.sum(b13[...], axis=0), 16) / D + EPS)
     whole(b14.at[pl.ds(0, NS - 1)], 14).wait_recv()
     last_sq = jnp.zeros((16, 1), F32)
     for t in range(NS):
-        last = bm[t, 0:16, :] + b14[t] * branch_scale * bm[t, 16:17, :]
+        last = bm[t, 0:16, :] + b14[t].astype(F32) * branch_scale * bm[t, 16:17, :]
         last_sq = last_sq + jnp.sum(last * last, axis=-1, keepdims=True)
         rows_f[:, t * WL:(t + 1) * WL] = last * bm[t, 17:18, :]
     s15[...] = column_to_row(last_sq)
-    other = {"guide": lax.rem(g + 1, 2)}
     send(s15, r15, 15, other)
-
-    full = nt_dot(rows_f[...].astype(BF16), emb[...])
-    high = full.astype(BF16)
-    low = (full - high.astype(F32)).astype(BF16)
-    logit = nn_dot(jnp.concatenate([high, low], axis=0), pick[...])
-    logit = logit[0:16, :] + logit[16:32, :]
+    pending.append((s15, 15, None))
+
+    logit = nn_dot(rows_f[...].astype(BF16), table[...])
     lower = jnp.concatenate([logit[0:4, :], logit[8:12, :]], axis=0)
     upper = jnp.concatenate([logit[4:8, :], logit[12:16, :]], axis=0)
     s16[...] = jnp.where(g == 0, upper, lower)
     send(s16, r16, 16, other)
+    pending.append((s16, 16, None))
     keep = jnp.where(g == 0, lower, upper)
     whole(r15, 15).wait_recv()
     lanes = iota((8, 128), 1)
@@ -400,42 +491,10 @@
         share = jnp.where(iota((4, 1), 0) == i, guidance[4 * g + i], share)
     whole(r16, 16).wait_recv()
     capped = LOGIT_CAP * jnp.tanh((keep + r16[...]) * final_scale / LOGIT_CAP)
-    out_ref[...] = capped[4:8, :] + share * (capped[0:4, :] - capped[4:8, :])
-
-    whole(s1.at[pl.ds(0, NP - 1)], 0).wait_send()
-    whole(b2.at[pl.ds(0, NP - 1)], 1).wait_send()
-
-    @pl.when(holds_tile)
-    def _():
-        whole(s3.at[pl.ds(0, NS - 1)], 2).wait_send()
-        for_out = s1.at[pl.ds(0, NP - 1), pl.ds(0, 8)]
-        whole(for_out, 3).wait_send()
-
-    @pl.when(jnp.logical_not(holds_tile))
-    def _():
-        whole(s3, 2).wait_send()
-
-    whole(b5.at[pl.ds(0, NKV - 1)], 4).wait_send()
-    whole(b6.at[pl.ds(0, NP - 1)], 5).wait_send()
-    whole(s8.at[pl.ds(0, NP - 1)], 6).wait_send()
-
-    @pl.when(holds_extra)
-    def _():
-        whole(s9.at[pl.ds(0, EXTRA - 1)], 7).wait_send()
-        whole(act.at[:, pl.ds(0, (NP - 1) * 128)], 11).wait_send()
-
-    @pl.when(jnp.logical_not(holds_extra))
-    def _():
-        whole(s9, 7).wait_send()
-
-    whole(b7.at[pl.ds(0, NP - 1)], 8).wait_send()
-    whole(bm.at[pl.ds(0, NS - 1)], 9).wait_send()
-    whole(act.at[:, pl.ds(0, (NP - 1) * FB)], 10).wait_send()
-    whole(b12.at[pl.ds(0, NKV - 1)], 12).wait_send()
-    whole(b13.at[pl.ds(0, NP - 1)], 13).wait_send()
-    whole(b14.at[pl.ds(0, NS - 1)], 14).wait_send()
-    whole(s15, 15).wait_send()
-    whole(s16, 16).wait_send()
+    base_ref[...] = capped[4:8, :]
+    lift_ref[...] = share * (capped[0:4, :] - capped[4:8, :])
+
+    finish()
 
 
 def on_device(
@@ -445,34 +504,33 @@
     gate_weight, up_weight, down_weight, embedding,
     cond_keys, cond_values, uncond_keys, uncond_values,
 ):
-    position = lengths.astype(F32)
-    frequency = THETA ** (-2.0 * jnp.arange(HD // 2, dtype=F32) / HD)
-    angles = position[:, :, None] * frequency
-    cosine = jnp.cos(angles)
-    sine = jnp.sin(angles)
-    cosine = jnp.concatenate([cosine, cosine], axis=-1)
-    sine = jnp.concatenate([-sine, sine], axis=-1)
-    gains = jnp.stack([pre_attn_gain, post_attn_gain, pre_ffw_gain, post_ffw_gain, final_gain])
+    lane = np.arange(HD) % (HD // 2)
+    freq = jnp.asarray((THETA ** (-2.0 * lane / HD)).astype(np.float32).reshape(1, HD))
+    gains = [
+        gain.reshape(1, WL)
+        for gain in (pre_attn_gain, post_attn_gain, pre_ffw_gain, post_ffw_gain, final_gain)
+    ]
     smem = pl.BlockSpec(memory_space=pltpu.SMEM)
     vmem = pl.BlockSpec(memory_space=pltpu.VMEM)
     hbm = pl.BlockSpec(memory_space=pl.ANY)
-    return pl.pallas_call(
+    base, lift = pl.pallas_call(
         step_kernel,
-        out_shape=jax.ShapeDtypeStruct((4, PICK), F32),
-        in_specs=[smem] * 3 + [vmem] * 5 + [hbm] * 12,
-        out_specs=vmem,
+        out_shape=[jax.ShapeDtypeStruct((4, PICK), F32)] * 2,
+        in_specs=[smem] * 3 + [vmem] * 8 + [hbm] * 12,
+        out_specs=[vmem] * 2,
         scratch_shapes=[
             pltpu.VMEM((WL, 2048), BF16),
-            pltpu.VMEM((1024, WL), BF16),
+            pltpu.VMEM((WL, 1024), BF16),
             pltpu.VMEM((WL, FFL), BF16),
             pltpu.VMEM((WL, FFL), BF16),
-            pltpu.VMEM((FFL, WL), BF16),
+            pltpu.VMEM((WL, FFL), BF16),
             pltpu.VMEM((ROWS, HALF), BF16),
             pltpu.VMEM((8, 256, 512), BF16),
             pltpu.VMEM((8, 256, 512), BF16),
             pltpu.VMEM((8, 64, 512), BF16),
             pltpu.VMEM((8, 64, 512), BF16),
             pltpu.VMEM((ROWS, PICK), BF16),
+            pltpu.VMEM((HALF, PICK), BF16),
             pltpu.VMEM((16, 8, 128), F32),
             pltpu.VMEM((16, 8, 128), F32),
             pltpu.VMEM((16, 8, 128), F32),
@@ -484,34 +542,46 @@
             pltpu.VMEM((NP, 9, 128), F32),
             pltpu.VMEM((16, 8, 128), F32),
             pltpu.VMEM((NKV, 16, WL), F32),
-            pltpu.VMEM((NP, 1, 128), F32),
+            pltpu.VMEM((NP, 4, 128), F32),
             pltpu.VMEM((NS, 18, WL), F32),
-            pltpu.VMEM((NP, 1, 128), F32),
-            pltpu.VMEM((NP, 16, 2 * FB), BF16),
-            pltpu.VMEM((NP, 16, 2 * FB), BF16),
-            pltpu.VMEM((EXTRA, 16, 256), BF16),
-            pltpu.VMEM((NP, 16, 256), BF16),
             pltpu.VMEM((16, FFL), BF16),
             pltpu.VMEM((NKV, 16, WL), F32),
             pltpu.VMEM((NP, 1, 128), F32),
-            pltpu.VMEM((NS, 16, WL), F32),
+            pltpu.VMEM((NS, 16, WL), BF16),
             pltpu.VMEM((8, PICK), F32),
             pltpu.VMEM((8, PICK), F32),
             pltpu.VMEM((1, 128), F32),
             pltpu.VMEM((1, 128), F32),
+            *[
+                pltpu.VMEM(shape, kind)
+                for _ in range(2)
+                for shape, kind in (
+                    ((NS, 16, 2 * FB), BF16),
+                    ((NS, 16, 2 * FB), BF16),
+                    ((NS, 16, 2 * FB), F32),
+                    ((NS, 16, 2 * FB), BF16),
+                    ((NS, 16, 2 * FB), BF16),
+                    ((4, 16, FB), BF16),
+                    ((4, 16, FB), BF16),
+                    ((4, 16, FB), F32),
+                    ((4, 16, FB), BF16),
+                    ((NS, 16, FB), BF16),
+                )
+            ],
             pltpu.SemaphoreType.DMA((12,)),
-            pltpu.SemaphoreType.DMA((17,)),
-            pltpu.SemaphoreType.DMA((17,)),
+            pltpu.SemaphoreType.DMA((24,)),
+            pltpu.SemaphoreType.DMA((24,)),
         ],
         compiler_params=pltpu.CompilerParams(
             collective_id=0, has_side_effects=True, vmem_limit_bytes=60 * 1024 * 1024
         ),
         name="decode_step",
     )(
-        lengths, slot_owner, guidance, hidden, allowed_ids.reshape(8, 128), cosine, sine, gains,
-        query_weight, key_weight, value_weight, output_weight, gate_weight, up_weight, down_weight,
+        lengths, slot_owner, guidance, hidden, allowed_ids.reshape(8, 128), freq, *gains,
+        query_weight, key_weight, value_weight, output_weight.T, gate_weight, up_weight, down_weight.T,
         embedding, cond_keys, cond_values, uncond_keys, uncond_values,
     )
+    return base + lift
 
 
 def solution(mesh):

time: 88.1 us -> 67 us (0.76)
  local copies, waits for them, and re-layouts: 10.4 us -> 0 us
  Pallas kernels: 75.8 us -> 65.4 us
    pallas_call x1, Pallas kernels: 75.8 us -> 65.4 us  [on_device(): pl.pallas_call(step_kernel, out_shape=[jax.ShapeDtypeStruct((4, PICK), F3...]
    unnamed x3 -> x0, local copies, waits for them, and re-layouts: 9.09 us -> none
    add x0 -> x1, other arithmetic: none -> 1.35 us  [on_device(): return base + lift]
    another operation x1 -> x0, local copies, waits for them, and re-layouts: 1.34 us -> none  [on_device(): jnp.stack([pre_attn_gain, post_attn_gain, pre_ffw_gain, post_ffw_gain, fi...]
where the time goes in v2:
time: 67 us; the launch traced here: 66.8 us
  Pallas kernels  65.4 us (98%)
  other arithmetic  1.35 us (2%)
    pallas_call x1, Pallas kernels, on_device(): pl.pallas_call(step_kernel, out_shape=[jax.ShapeDtypeStruct((4, PICK), F3...  65.4 us
    add x1, other arithmetic, on_device(): return base + lift  1.35 us

profile of v2, /device:TPU:1, one launch (start us, length us, event | category | flops | bytes accessed | tf_op | source)
XLA Modules:
  0.0 66.8 jit_solution(9591681187249237061)
XLA Ops:
  0.0 65.4 %decode_step.1 = (f32[4,1024]{1,0:T(4,128)}, f32[4,1024]{1,0:T(4,128)}) custom-call(s32[2,8]{1,0:T(2,128)} %lengths.1, s32[2,8]{1,0:T(2,128)} %owner.1, f32[8]{0:T(128)} %guidance.1, bf16[2,8,144]{2,1,0:T(8,128)(2,1)} %hidden.1, s32[8,128]{1,0:T(8,128)} %bitcast.10, f32[1,128]{1,0:T(1,128)} %constant.2.clone.freq, f32[1,144]{1,0:T(1,128)} %bitcast.11, ...), custom_call_target="tpu_custom_call" | custom-call | tf_op jit(solution)/shard_map/decode_step/pallas_call | solution.py:516
  65.4 1.3 %add.3 = f32[4,1024]{1,0:T(4,128)} add(f32[4,1024]{1,0:T(4,128)} %get-tuple-element.7, f32[4,1024]{1,0:T(4,128)} %get-tuple-element.8) | non-fusion elementwise | flops 4096 | bytes 49152 | tf_op jit(solution)/shard_map/add | solution.py:584

commit v3 on v2

--- a/solution.py
+++ b/solution.py
@@ -58,13 +58,14 @@
 
 
 def step_kernel(
-    lengths, owner, guidance, hidden, ids, freq, gain0, gain1, gain2, gain3, gain4,
+    lengths_h, owner_h, guidance_h, hidden_h, ids_h, freq_h, gain0_h, gain1_h, gain2_h, gain3_h, gain4_h,
     qw_h, kw_h, vw_h, ow_h, gw_h, uw_h, dw_h, emb_h, ck_h, cv_h, uk_h, uv_h,
     base_ref, lift_ref,
     w_qkv, w_o, w_g, w_u, w_d, emb, ck, cv, uk, uv,
     pick, table, qs, ks, vs, rows_f,
-    s1, r1, b2, s3, r3, b4, b5, b6, bm, act, b12, b13, b14, s16, r16, s15, r15,
+    s1, r1, b2, s3, r3, b4, b5, b6, bm, act, b12, b13, b14, s16, r16,
     pa, qa, ka, sa, ra, ta, ua, va, wa, xa, pb, qb, kb, sb, rb, tb, ub, vb, wb, xb,
+    lengths, owner, guidance, hidden, ids, freq, gain0, gain1, gain2, gain3, gain4,
     load_sem, send_sem, recv_sem,
 ):
     g = lax.axis_index("guide")
@@ -90,11 +91,20 @@
                 (uw_h, w_u),
                 (dw_h, w_d),
                 (emb_h, emb),
+                (hidden_h, hidden),
+                (gain0_h, gain0),
+                (lengths_h, lengths),
+                (owner_h, owner),
+                (guidance_h, guidance),
+                (ids_h, ids),
+                (freq_h, freq),
+                (gain1_h, gain1),
+                (gain2_h, gain2),
+                (gain3_h, gain3),
+                (gain4_h, gain4),
             ]
         )
     ]
-    for load in loads[0:3]:
-        load.start()
 
     def peer(off):
         g2 = lax.rem(g + lax.div(off, 16), 2)
@@ -140,6 +150,8 @@
         barrier, inc=1, device_id={"guide": g2, "seq": s2}, device_id_type=MESH))
     to_kv(lambda k2: pl.semaphore_signal(barrier, inc=1, device_id={"kv": k2}, device_id_type=MESH))
 
+    for load in loads[12:23] + loads[0:3]:
+        load.start()
     other = {"guide": lax.rem(g + 1, 2)}
     tail = NP * FB
     holds_extra = (lax.rem(x, 2) == lax.rem(z, 2)) & (lax.div(z, 2) == g)
@@ -200,6 +212,8 @@
         pending.append((tail_out.at[pl.ds(0, 3)], base + 1, holds_extra))
         pending.append((tail_out, base + 1, jnp.logical_not(holds_extra)))
 
+    for load in loads[12:23]:
+        load.wait()
     x_in = hidden[...].astype(F32).reshape(16, WL)
     normed = (x_in * gain0[...]).astype(BF16)
     x_sq = column_to_row(jnp.sum(x_in * x_in, axis=-1, keepdims=True))
@@ -382,13 +396,13 @@
     whole(b5.at[pl.ds(0, NKV - 1)], 4).wait_recv()
     projected = (b5[0] + b5[1]) + (b5[2] + b5[3])
     branch = projected * gain1[...]
+    ffw_product(branch * gain2[...], set_b, 19)
     b6[me, 0:1, :] = column_to_row(jnp.sum(projected * projected, axis=-1, keepdims=True))
     b6[me, 1:2, :] = column_to_row(jnp.sum(x_in * branch, axis=-1, keepdims=True))
     b6[me, 2:3, :] = column_to_row(jnp.sum(branch * branch, axis=-1, keepdims=True))
     b6[me, 3:4, :] = x_sq
     to_plane(lambda g2, s2: send(b6.at[me], b6.at[me], 5, {"guide": g2, "seq": s2}))
     pending.append((b6.at[pl.ds(0, NP - 1)], 5, None))
-    ffw_product(branch * gain2[...], set_b, 19)
     ffw_combine(set_b, 19)
     ffw_send(set_b, 21)
     pick_table(4, 3)
@@ -463,34 +477,32 @@
     whole(b13.at[pl.ds(0, NP - 1)], 13).wait_recv()
     branch_scale = lax.rsqrt(row_to_column(jnp.sum(b13[...], axis=0), 16) / D + EPS)
     whole(b14.at[pl.ds(0, NS - 1)], 14).wait_recv()
-    last_sq = jnp.zeros((16, 1), F32)
+    last_sq = jnp.zeros((16, WL), F32)
     for t in range(NS):
         last = bm[t, 0:16, :] + b14[t].astype(F32) * branch_scale * bm[t, 16:17, :]
-        last_sq = last_sq + jnp.sum(last * last, axis=-1, keepdims=True)
+        last_sq = last_sq + last * last
         rows_f[:, t * WL:(t + 1) * WL] = last * bm[t, 17:18, :]
-    s15[...] = column_to_row(last_sq)
-    send(s15, r15, 15, other)
-    pending.append((s15, 15, None))
+    sq_row = column_to_row(jnp.sum(last_sq, axis=-1, keepdims=True))
 
     logit = nn_dot(rows_f[...].astype(BF16), table[...])
     lower = jnp.concatenate([logit[0:4, :], logit[8:12, :]], axis=0)
     upper = jnp.concatenate([logit[4:8, :], logit[12:16, :]], axis=0)
-    s16[...] = jnp.where(g == 0, upper, lower)
+    s16[0:8, :] = jnp.where(g == 0, upper, lower)
+    s16[8:9, 0:128] = sq_row
     send(s16, r16, 16, other)
     pending.append((s16, 16, None))
     keep = jnp.where(g == 0, lower, upper)
-    whole(r15, 15).wait_recv()
+    whole(r16, 16).wait_recv()
     lanes = iota((8, 128), 1)
     rowi = iota((8, 128), 0)
     want = lax.div(rowi, 4) * 8 + 4 * g + lax.rem(rowi, 4)
-    sq = jnp.sum(jnp.where(lanes == want, jnp.broadcast_to(s15[...] + r15[...], (8, 128)), 0.0),
+    sq = jnp.sum(jnp.where(lanes == want, jnp.broadcast_to(sq_row + r16[8:9, 0:128], (8, 128)), 0.0),
                  axis=1, keepdims=True)
     final_scale = lax.rsqrt(sq / D + EPS)
     share = jnp.zeros((4, 1), F32)
     for i in range(4):
         share = jnp.where(iota((4, 1), 0) == i, guidance[4 * g + i], share)
-    whole(r16, 16).wait_recv()
-    capped = LOGIT_CAP * jnp.tanh((keep + r16[...]) * final_scale / LOGIT_CAP)
+    capped = LOGIT_CAP * jnp.tanh((keep + r16[0:8, :]) * final_scale / LOGIT_CAP)
     base_ref[...] = capped[4:8, :]
     lift_ref[...] = share * (capped[0:4, :] - capped[4:8, :])
 
@@ -510,13 +522,12 @@
         gain.reshape(1, WL)
         for gain in (pre_attn_gain, post_attn_gain, pre_ffw_gain, post_ffw_gain, final_gain)
     ]
-    smem = pl.BlockSpec(memory_space=pltpu.SMEM)
     vmem = pl.BlockSpec(memory_space=pltpu.VMEM)
     hbm = pl.BlockSpec(memory_space=pl.ANY)
     base, lift = pl.pallas_call(
         step_kernel,
         out_shape=[jax.ShapeDtypeStruct((4, PICK), F32)] * 2,
-        in_specs=[smem] * 3 + [vmem] * 8 + [hbm] * 12,
+        in_specs=[hbm] * 23,
         out_specs=[vmem] * 2,
         scratch_shapes=[
             pltpu.VMEM((WL, 2048), BF16),
@@ -548,10 +559,8 @@
             pltpu.VMEM((NKV, 16, WL), F32),
             pltpu.VMEM((NP, 1, 128), F32),
             pltpu.VMEM((NS, 16, WL), BF16),
-            pltpu.VMEM((8, PICK), F32),
-            pltpu.VMEM((8, PICK), F32),
-            pltpu.VMEM((1, 128), F32),
-            pltpu.VMEM((1, 128), F32),
+            pltpu.VMEM((9, PICK), F32),
+            pltpu.VMEM((9, PICK), F32),
             *[
                 pltpu.VMEM(shape, kind)
                 for _ in range(2)
@@ -568,7 +577,14 @@
                     ((NS, 16, FB), BF16),
                 )
             ],
-            pltpu.SemaphoreType.DMA((12,)),
+            pltpu.SMEM((2, 8), jnp.int32),
+            pltpu.SMEM((2, 8), jnp.int32),
+            pltpu.SMEM((8,), F32),
+            pltpu.VMEM((2, 8, WL), BF16),
+            pltpu.VMEM((8, 128), jnp.int32),
+            pltpu.VMEM((1, HD), F32),
+            *[pltpu.VMEM((1, WL), F32)] * 5,
+            pltpu.SemaphoreType.DMA((23,)),
             pltpu.SemaphoreType.DMA((24,)),
             pltpu.SemaphoreType.DMA((24,)),
         ],

time: 67 us -> 65.5 us (0.978)
  Pallas kernels: 65.4 us -> 64 us
    pallas_call x1, Pallas kernels: 65.4 us -> 64 us  [on_device(): pl.pallas_call(step_kernel, out_shape=[jax.ShapeDtypeStruct((4, PICK), F3...]
where the time goes in v3:
time: 65.5 us; the launch traced here: 65.3 us
  Pallas kernels  64 us (98%)
  other arithmetic  1.35 us (2%)
    pallas_call x1, Pallas kernels, on_device(): pl.pallas_call(step_kernel, out_shape=[jax.ShapeDtypeStruct((4, PICK), F3...  64 us
    add x1, other arithmetic, on_device(): return base + lift  1.35 us

profile of v3, /device:TPU:1, one launch (start us, length us, event | category | flops | bytes accessed | tf_op | source)
XLA Modules:
  0.0 65.3 jit_solution(16366836332598009199)
XLA Ops:
  0.0 64.0 %decode_step.1 = (f32[4,1024]{1,0:T(4,128)}, f32[4,1024]{1,0:T(4,128)}) custom-call(s32[2,8]{1,0:T(2,128)} %lengths_h.1, s32[2,8]{1,0:T(2,128)} %owner_h.1, f32[8]{0:T(128)} %guidance_h.1, bf16[2,8,144]{2,1,0:T(8,128)(2,1)} %hidden_h.1, s32[8,128]{1,0:T(8,128)} %bitcast.10, f32[1,128]{1,0:T(1,128)} %constant.2.clone.freq_h, f32[1,144]{1,0:T(1,128)} %bitcast.11, ...), custom_call_target="tpu_custom_call" | custom-call | tf_op jit(solution)/shard_map/decode_step/pallas_call | solution.py:527
  64.0 1.3 %add.3 = f32[4,1024]{1,0:T(4,128)} add(f32[4,1024]{1,0:T(4,128)} %get-tuple-element.7, f32[4,1024]{1,0:T(4,128)} %get-tuple-element.8) | non-fusion elementwise | flops 4096 | bytes 49152 | tf_op jit(solution)/shard_map/add | solution.py:600

commit v4 on v3

--- a/solution.py
+++ b/solution.py
@@ -63,7 +63,7 @@
     base_ref, lift_ref,
     w_qkv, w_o, w_g, w_u, w_d, emb, ck, cv, uk, uv,
     pick, table, qs, ks, vs, rows_f,
-    s1, r1, b2, s3, r3, b4, b5, b6, bm, act, b12, b13, b14, s16, r16,
+    s1, r1, b2, s3, r3, b4, b6, bm, act, b12, b13, b14, s16, r16,
     pa, qa, ka, sa, ra, ta, ua, va, wa, xa, pb, qb, kb, sb, rb, tb, ub, vb, wb, xb,
     lengths, owner, guidance, hidden, ids, freq, gain0, gain1, gain2, gain3, gain4,
     load_sem, send_sem, recv_sem,
@@ -86,7 +86,7 @@
                 (uk_h, uk),
                 (cv_h, cv),
                 (uv_h, uv),
-                (ow_h, w_o),
+                (ow_h, w_o.at[kv]),
                 (gw_h, w_g),
                 (uw_h, w_u),
                 (dw_h, w_d),
@@ -219,8 +219,8 @@
     x_sq = column_to_row(jnp.sum(x_in * x_in, axis=-1, keepdims=True))
     for i in range(3):
         loads[i].wait()
-    for load in loads[3:12]:
-        load.start()
+    for i in (8, 9, 3, 4, 7, 5, 6, 11, 10):
+        loads[i].start()
     part = nn_dot(normed, w_qkv[...])
     for j in range(NS):
         for k in range(NG):
@@ -260,7 +260,11 @@
         s1.at[g2 * NS + s2], r1.at[me], 0, {"guide": g2, "seq": s2}))
     pending.append((s1.at[pl.ds(0, NP - 1)], 0, None))
 
+    loads[8].wait()
+    loads[9].wait()
+    ffw_product(x_in * gain2[...], set_a, 6)
     lax.fori_loop(0, ROWS // 256, pick_rows, 0)
+    ffw_combine(set_a, 6)
     whole(r1.at[pl.ds(0, NP - 1)], 0).wait_recv()
     total = jnp.sum(r1[...], axis=0)
     scale = lax.rsqrt(row_to_column(total[8:9, :], 8, 8 * g) / D + EPS)
@@ -271,6 +275,10 @@
     b2[me] = y.astype(BF16).astype(F32)
     to_plane(lambda g2, s2: send(b2.at[me], b2.at[me], 1, {"guide": g2, "seq": s2}))
     pending.append((b2.at[pl.ds(0, NP - 1)], 1, None))
+    ffw_send(set_a, 17)
+    loads[7].wait()
+    to_kv(lambda k2: send(w_o.at[kv], w_o.at[kv], 4, {"kv": k2}))
+    pending.append((w_o.at[pl.ds(0, NKV - 1)], 4, None))
 
     picks = []
     r_ = iota((64, 128), 0)
@@ -296,9 +304,6 @@
             limit = jnp.where(row == j, lengths[k, owner[k, j]], limit)
         limits.append(iota((64, span), 1) + block * span < limit)
 
-    loads[8].wait()
-    loads[9].wait()
-    ffw_product(x_in * gain2[...], set_a, 6)
     for i in range(3, 7):
         loads[i].wait()
     whole(b2.at[pl.ds(0, NP - 1)], 1).wait_recv()
@@ -341,7 +346,7 @@
 
     pending.append((s3.at[pl.ds(0, NS - 1)], 2, holds_tile))
     pending.append((s3, 2, jnp.logical_not(holds_tile)))
-    pending.append((s1.at[pl.ds(0, NP - 1), pl.ds(0, 8)], 3, holds_tile))
+    pending.append((table.at[pl.ds(0, (NP * NKV - 1) * 8), pl.ds(0, 128)], 3, holds_tile))
 
     for k in range(NG):
         kx = nn_dot(picks[k][1], gathered[k])
@@ -350,7 +355,6 @@
             ks[k * 8 + j] = kx[j * 8:(j + 1) * 8, :]
             vs[k * 8 + j] = vx[j * 8:(j + 1) * 8, :]
 
-    ffw_combine(set_a, 6)
     loads[11].wait()
     pick_table(0, 1)
 
@@ -362,8 +366,16 @@
         sums = jnp.sum(r3[...], axis=0)
         numer = sums[0:8, :] + own.astype(BF16).astype(F32) * vs[s]
         den = row_to_column(sums[8:9, :], 8) + own
-        b4[s] = (numer / den).astype(BF16).astype(F32)
-        to_plane(lambda g2, s2: send(b4.at[s], b4.at[s], 3, {"guide": g2, "seq": s2}))
+        at = kv * NS + s
+        b4[at] = (numer / den).astype(BF16)
+
+        def to_all(off, carry):
+            g2, s2 = peer(lax.rem(off, NP))
+            k2 = lax.rem(kv + lax.div(off, NP), NKV)
+            send(b4.at[at], b4.at[at], 3, {"guide": g2, "kv": k2, "seq": s2})
+            return carry
+
+        lax.fori_loop(1, NP * NKV, to_all, 0)
 
     r_ = iota((128, 128), 0)
     c_ = iota((128, 128), 1)
@@ -375,26 +387,23 @@
         & (lax.rem(lax.div(r_, 8), 2) == lax.div(c_, 64))
         & (lax.rem(r_, 8) == held)
     )
-    pick_table(1, 2)
-    loads[7].wait()
+    pick_table(1, 3)
+    whole(w_o.at[pl.ds(0, NKV - 1)], 4).wait_recv()
 
     @pl.when(holds_tile)
     def _():
-        whole(b4.at[pl.ds(0, NS - 1)], 3).wait_recv()
+        whole(b4.at[pl.ds(0, NKV * NS - 1)], 3).wait_recv()
 
     @pl.when(jnp.logical_not(holds_tile))
     def _():
         whole(b4, 3).wait_recv()
 
-    att = nn_dot(back, b4[...].reshape(128, 128).astype(BF16))
-    att = jnp.concatenate([att[h * 16:(h + 1) * 16, :] for h in range(8)], axis=1).astype(BF16)
-    b5[kv] = nt_dot(att, w_o[...])
-    to_kv(lambda k2: send(b5.at[kv], b5.at[kv], 4, {"kv": k2}))
-    pending.append((b5.at[pl.ds(0, NKV - 1)], 4, None))
-    ffw_send(set_a, 17)
-    pick_table(3, 1)
-    whole(b5.at[pl.ds(0, NKV - 1)], 4).wait_recv()
-    projected = (b5[0] + b5[1]) + (b5[2] + b5[3])
+    projected = jnp.zeros((16, WL), F32)
+    for k in range(NKV):
+        tiles = b4[k * NS:(k + 1) * NS].astype(F32).reshape(128, 128).astype(BF16)
+        att = nn_dot(back, tiles)
+        att = jnp.concatenate([att[h * 16:(h + 1) * 16, :] for h in range(8)], axis=1).astype(BF16)
+        projected = projected + nt_dot(att, w_o[k])
     branch = projected * gain1[...]
     ffw_product(branch * gain2[...], set_b, 19)
     b6[me, 0:1, :] = column_to_row(jnp.sum(projected * projected, axis=-1, keepdims=True))
@@ -531,7 +540,7 @@
         out_specs=[vmem] * 2,
         scratch_shapes=[
             pltpu.VMEM((WL, 2048), BF16),
-            pltpu.VMEM((WL, 1024), BF16),
+            pltpu.VMEM((NKV, WL, 1024), BF16),
             pltpu.VMEM((WL, FFL), BF16),
             pltpu.VMEM((WL, FFL), BF16),
             pltpu.VMEM((WL, FFL), BF16),
@@ -551,8 +560,7 @@
             pltpu.VMEM((NP, 8, 128), F32),
             pltpu.VMEM((16, 9, 128), F32),
             pltpu.VMEM((NP, 9, 128), F32),
-            pltpu.VMEM((16, 8, 128), F32),
-            pltpu.VMEM((NKV, 16, WL), F32),
+            pltpu.VMEM((NKV * NS, 8, 128), BF16),
             pltpu.VMEM((NP, 4, 128), F32),
             pltpu.VMEM((NS, 18, WL), F32),
             pltpu.VMEM((16, FFL), BF16),

time: 65.5 us -> 66.5 us (1.015)
  Pallas kernels: 64 us -> 64.9 us
    pallas_call x1, Pallas kernels: 64 us -> 64.9 us  [on_device(): pl.pallas_call(step_kernel, out_shape=[jax.ShapeDtypeStruct((4, PICK), F3...]
where the time goes in v4:
time: 66.5 us; the launch traced here: 66.2 us
  Pallas kernels  64.9 us (98%)
  other arithmetic  1.35 us (2%)
    pallas_call x1, Pallas kernels, on_device(): pl.pallas_call(step_kernel, out_shape=[jax.ShapeDtypeStruct((4, PICK), F3...  64.9 us
    add x1, other arithmetic, on_device(): return base + lift  1.35 us

profile of v4, /device:TPU:1, one launch (start us, length us, event | category | flops | bytes accessed | tf_op | source)
XLA Modules:
  0.0 66.2 jit_solution(4813676067033402635)
XLA Ops:
  0.0 64.9 %decode_step.1 = (f32[4,1024]{1,0:T(4,128)}, f32[4,1024]{1,0:T(4,128)}) custom-call(s32[2,8]{1,0:T(2,128)} %lengths_h.1, s32[2,8]{1,0:T(2,128)} %owner_h.1, f32[8]{0:T(128)} %guidance_h.1, bf16[2,8,144]{2,1,0:T(8,128)(2,1)} %hidden_h.1, s32[8,128]{1,0:T(8,128)} %bitcast.10, f32[1,128]{1,0:T(1,128)} %constant.2.clone.freq_h, f32[1,144]{1,0:T(1,128)} %bitcast.11, ...), custom_call_target="tpu_custom_call" | custom-call | tf_op jit(solution)/shard_map/decode_step/pallas_call | solution.py:536
  64.9 1.3 %add.3 = f32[4,1024]{1,0:T(4,128)} add(f32[4,1024]{1,0:T(4,128)} %get-tuple-element.7, f32[4,1024]{1,0:T(4,128)} %get-tuple-element.8) | non-fusion elementwise | flops 4096 | bytes 49152 | tf_op jit(solution)/shard_map/add | solution.py:608

commit v5 on v3

--- a/solution.py
+++ b/solution.py
@@ -268,7 +268,7 @@
     turned = y * cosine + pltpu.roll(y, 64, 1) * sine
     y = jnp.where(s < 12, turned, y)
     y = jnp.where(s < 8, y * (D // H) ** (-0.5), y)
-    b2[me] = y.astype(BF16).astype(F32)
+    b2[me] = y.astype(BF16)
     to_plane(lambda g2, s2: send(b2.at[me], b2.at[me], 1, {"guide": g2, "seq": s2}))
     pending.append((b2.at[pl.ds(0, NP - 1)], 1, None))
 
@@ -302,8 +302,22 @@
     for i in range(3, 7):
         loads[i].wait()
     whole(b2.at[pl.ds(0, NP - 1)], 1).wait_recv()
-    gathered = b2[...].reshape(NG, 128, 128).astype(BF16)
+    gathered = b2[...].astype(F32).reshape(NG, 128, 128).astype(BF16)
     lane_head = lax.div(lax.rem(iota((64, 128), 0), 8), 2)
+    holds_tile = g == lax.rem(s, 2)
+
+    def send_tiles(first):
+        def one(off, carry):
+            i = first + lax.rem(s + off, 8)
+
+            @pl.when(jnp.logical_or(i != s, jnp.logical_not(holds_tile)))
+            def _():
+                send(s3.at[i], r3.at[me], 2, {"guide": lax.rem(i, 2), "seq": i})
+
+            return carry
+
+        lax.fori_loop(0, 8, one, 0)
+
     for k, span, keys, values in ((0, 256, ck, cv), (1, 64, uk, uv)):
         q = nn_dot(picks[k][0], gathered[k])
         for j in range(8):
@@ -324,24 +338,11 @@
                 mine = jnp.where(lane_head[0:8, :] == b, full[:, b * 128:(b + 1) * 128], mine)
             s3[k * 8 + j, 0:8, :] = mine
             s3[k * 8 + j, 8:9, :] = column_to_row(denom[j * 8:(j + 1) * 8, :])
-
-    tile_guide = lax.rem(s, 2)
-    holds_tile = g == tile_guide
-
-    def send_tile(off, carry):
-        i = lax.rem(s + off, NS)
-        send(s3.at[i], r3.at[me], 2, {"guide": lax.rem(i, 2), "seq": i})
-        return carry
-
-    lax.fori_loop(1, NS, send_tile, 0)
-
-    @pl.when(jnp.logical_not(holds_tile))
-    def _():
-        send(s3.at[s], r3.at[me], 2, {"guide": tile_guide, "seq": s})
+        send_tiles(k * 8)
 
     pending.append((s3.at[pl.ds(0, NS - 1)], 2, holds_tile))
     pending.append((s3, 2, jnp.logical_not(holds_tile)))
-    pending.append((s1.at[pl.ds(0, NP - 1), pl.ds(0, 8)], 3, holds_tile))
+    pending.append((b2.at[pl.ds(0, NP - 1)], 3, holds_tile))
 
     for k in range(NG):
         kx = nn_dot(picks[k][1], gathered[k])
@@ -362,7 +363,7 @@
         sums = jnp.sum(r3[...], axis=0)
         numer = sums[0:8, :] + own.astype(BF16).astype(F32) * vs[s]
         den = row_to_column(sums[8:9, :], 8) + own
-        b4[s] = (numer / den).astype(BF16).astype(F32)
+        b4[s] = (numer / den).astype(BF16)
         to_plane(lambda g2, s2: send(b4.at[s], b4.at[s], 3, {"guide": g2, "seq": s2}))
 
     r_ = iota((128, 128), 0)
@@ -386,7 +387,7 @@
     def _():
         whole(b4, 3).wait_recv()
 
-    att = nn_dot(back, b4[...].reshape(128, 128).astype(BF16))
+    att = nn_dot(back, b4[...].astype(F32).reshape(128, 128).astype(BF16))
     att = jnp.concatenate([att[h * 16:(h + 1) * 16, :] for h in range(8)], axis=1).astype(BF16)
     b5[kv] = nt_dot(att, w_o[...])
     to_kv(lambda k2: send(b5.at[kv], b5.at[kv], 4, {"kv": k2}))
@@ -430,11 +431,8 @@
     whole(ra.at[pl.ds(0, NS - 1)], 17).wait_recv()
     first = gathered_sum(ra)
     whole(rb.at[pl.ds(0, NS - 1)], 21).wait_recv()
-    mine = pl.ds(pl.multiple_of(me * FB, FB), FB)
-    act[:, mine] = activate(first, gathered_sum(rb))
-    to_plane(lambda g2, s2: send(act.at[:, mine], act.at[:, mine], 10, {"guide": g2, "seq": s2}))
-    pending.append((act.at[:, pl.ds(0, (NP - 1) * FB)], 10, None))
-    pending.append((act.at[:, pl.ds(0, (NP - 1) * 128)], 11, holds_extra))
+    main = activate(first, gathered_sum(rb))
+    act[me, :, 0:FB] = main
 
     @pl.when(holds_extra)
     def _():
@@ -443,25 +441,38 @@
         xb[s] = wb[own]
         whole(xa.at[pl.ds(0, NS - 1)], 18).wait_recv()
         whole(xb.at[pl.ds(0, NS - 1)], 22).wait_recv()
-        cols = pl.ds(pl.multiple_of(tail + extra * 128, 128), 128)
-        act[:, cols] = activate(gathered_sum(xa), gathered_sum(xb))
-        to_plane(lambda g2, s2: send(act.at[:, cols], act.at[:, cols], 11, {"guide": g2, "seq": s2}))
+        act[me, :, FB:FB + 128] = activate(gathered_sum(xa), gathered_sum(xb))
+        to_plane(lambda g2, s2: send(act.at[me], act.at[me], 10, {"guide": g2, "seq": s2}))
+
+    @pl.when(jnp.logical_not(holds_extra))
+    def _():
+        to_plane(lambda g2, s2: send(
+            act.at[me, :, pl.ds(0, FB)], act.at[me, :, pl.ds(0, FB)], 10, {"guide": g2, "seq": s2}))
+
+    pending.append((act.at[pl.ds(0, NP - 1)], 10, holds_extra))
+    pending.append((act.at[pl.ds(0, NP - 1), :, pl.ds(0, FB)], 10, jnp.logical_not(holds_extra)))
 
     pick_table(7, 2)
     loads[10].wait()
-    whole(act.at[:, pl.ds(0, (NP - 1) * FB)], 10).wait_recv()
+    blocks = 2 * (NP - 1) + EXTRA
 
     @pl.when(holds_extra)
     def _():
-        whole(act.at[:, pl.ds(0, (EXTRA - 1) * 128)], 11).wait_recv()
+        whole(table.at[pl.ds(0, (blocks - 1) * 16), pl.ds(0, 128)], 10).wait_recv()
 
     @pl.when(jnp.logical_not(holds_extra))
     def _():
-        whole(act.at[:, pl.ds(0, EXTRA * 128)], 11).wait_recv()
+        whole(table.at[pl.ds(0, blocks * 16), pl.ds(0, 128)], 10).wait_recv()
 
     to_plane(lambda g2, s2: send(bm.at[s], bm.at[s], 9, {"seq": s2}), NS)
     pending.append((bm.at[pl.ds(0, NS - 1)], 9, None))
-    b12[kv] = nt_dot(act[...], w_d[...])
+    owners = []
+    for e in range(EXTRA):
+        z2 = e // 2
+        owners.append((e // 4) * NS + 4 * z2 + 2 * (e % 2) + z2 % 2)
+    hidden_units = jnp.concatenate(
+        [act[r, :, 0:FB] for r in range(NP)] + [act[r, :, FB:FB + 128] for r in owners], axis=1)
+    b12[kv] = nt_dot(hidden_units, w_d[...])
     to_kv(lambda k2: send(b12.at[kv], b12.at[kv], 12, {"kv": k2}))
     pending.append((b12.at[pl.ds(0, NKV - 1)], 12, None))
     whole(b12.at[pl.ds(0, NKV - 1)], 12).wait_recv()
@@ -548,14 +559,14 @@
             pltpu.VMEM((16, HALF), F32),
             pltpu.VMEM((NP, 9, 128), F32),
             pltpu.VMEM((NP, 9, 128), F32),
-            pltpu.VMEM((NP, 8, 128), F32),
+            pltpu.VMEM((NP, 8, 128), BF16),
             pltpu.VMEM((16, 9, 128), F32),
             pltpu.VMEM((NP, 9, 128), F32),
-            pltpu.VMEM((16, 8, 128), F32),
+            pltpu.VMEM((16, 8, 128), BF16),
             pltpu.VMEM((NKV, 16, WL), F32),
             pltpu.VMEM((NP, 4, 128), F32),
             pltpu.VMEM((NS, 18, WL), F32),
-            pltpu.VMEM((16, FFL), BF16),
+            pltpu.VMEM((NP, 16, FB + 128), BF16),
             pltpu.VMEM((NKV, 16, WL), F32),
             pltpu.VMEM((NP, 1, 128), F32),
             pltpu.VMEM((NS, 16, WL), BF16),

time: 65.5 us -> 65.3 us (level)
  no operation moved by 1% of the time
where the time goes in v5:
time: 65.3 us; the launch traced here: 65 us
  Pallas kernels  63.7 us (98%)
  other arithmetic  1.35 us (2%)
    pallas_call x1, Pallas kernels, on_device(): pl.pallas_call(step_kernel, out_shape=[jax.ShapeDtypeStruct((4, PICK), F3...  63.7 us
    add x1, other arithmetic, on_device(): return base + lift  1.35 us

profile of v5, /device:TPU:1, one launch (start us, length us, event | category | flops | bytes accessed | tf_op | source)
XLA Modules:
  0.0 65.0 jit_solution(9469394674925044761)
XLA Ops:
  0.0 63.7 %decode_step.1 = (f32[4,1024]{1,0:T(4,128)}, f32[4,1024]{1,0:T(4,128)}) custom-call(s32[2,8]{1,0:T(2,128)} %lengths_h.1, s32[2,8]{1,0:T(2,128)} %owner_h.1, f32[8]{0:T(128)} %guidance_h.1, bf16[2,8,144]{2,1,0:T(8,128)(2,1)} %hidden_h.1, s32[8,128]{1,0:T(8,128)} %bitcast.10, f32[1,128]{1,0:T(1,128)} %constant.2.clone.freq_h, f32[1,144]{1,0:T(1,128)} %bitcast.11, ...), custom_call_target="tpu_custom_call" | custom-call | tf_op jit(solution)/shard_map/decode_step/pallas_call | solution.py:538
  63.7 1.3 %add.3 = f32[4,1024]{1,0:T(4,128)} add(f32[4,1024]{1,0:T(4,128)} %get-tuple-element.7, f32[4,1024]{1,0:T(4,128)} %get-tuple-element.8) | non-fusion elementwise | flops 4096 | bytes 49152 | tf_op jit(solution)/shard_map/add | solution.py:611

commit v6 on v5

--- a/solution.py
+++ b/solution.py
@@ -159,8 +159,10 @@
     set_a = (pa, qa, ka, sa, ra, ta, ua, va, wa, xa)
     set_b = (pb, qb, kb, sb, rb, tb, ub, vb, wb, xb)
 
-    def ffw_product(rows, buffers, base):
-        away, _, keep, _, _, tail_away, _, tail_keep, _, _ = buffers
+    parts = ((2, 1), (3, 0))
+
+    def ffw_product(rows, buffers, sems):
+        away, came, keep, _, _, tail_away, tail_came, tail_keep, _, _ = buffers
         high = rows.astype(BF16)
         low = (rows - high.astype(F32)).astype(BF16)
         both = jnp.concatenate([high, low], axis=0)
@@ -169,31 +171,55 @@
             wide = nn_dot(both, weight[:, cols])
             return wide[0:16, :] + wide[16:32, :]
 
-        for whose, main, rest in ((1 - g, away, tail_away), (g, keep, tail_keep)):
-            cols = pl.ds(pl.multiple_of(whose * (NS * FB), NS * FB), NS * FB)
-            tail_cols = pl.ds(pl.multiple_of(tail + whose * 512, 512), 512)
+        def chip_row(whose, into, dz):
+            first = 4 * lax.rem(z + dz, 4)
+            cols = pl.ds(pl.multiple_of((whose * NS + first) * FB, 4 * FB), 4 * FB)
             for at, weight in ((0, w_g), (1, w_u)):
-                part = product(weight, cols).astype(main.dtype)
-                for c in range(NS):
-                    main[c, :, at * FB:(at + 1) * FB] = part[:, c * FB:(c + 1) * FB]
-                part = product(weight, tail_cols).astype(rest.dtype)
+                part = product(weight, cols).astype(into.dtype)
                 for c in range(4):
-                    rest[c, :, at * 128:(at + 1) * 128] = part[:, c * 128:(c + 1) * 128]
-            if main is away:
-                send(away, buffers[1], base, other)
-                send(tail_away, buffers[6], base + 1, other)
-                pending.append((away, base, None))
-                pending.append((tail_away, base + 1, None))
-
-    def ffw_combine(buffers, base):
+                    into[first + c, :, at * FB:(at + 1) * FB] = part[:, c * FB:(c + 1) * FB]
+            return first
+
+        def tail_block(whose, into):
+            cols = pl.ds(pl.multiple_of(tail + whose * 512, 512), 512)
+            for at, weight in ((0, w_g), (1, w_u)):
+                part = product(weight, cols).astype(into.dtype)
+                for c in range(4):
+                    into[c, :, at * 128:(at + 1) * 128] = part[:, c * 128:(c + 1) * 128]
+
+        for i, pair in enumerate(parts):
+            for dz in pair:
+                first = chip_row(1 - g, away, dz)
+                send(away.at[pl.ds(first, 4)], came.at[pl.ds(first, 4)], sems[i], other)
+            pending.append((away.at[pl.ds(0, 8)], sems[i], None))
+        tail_block(1 - g, tail_away)
+        send(tail_away, tail_came, sems[2], other)
+        pending.append((tail_away, sems[2], None))
+        for pair in parts:
+            for dz in pair:
+                chip_row(g, keep, dz)
+        tail_block(g, tail_keep)
+
+    def ffw_combine(buffers, sems, i):
         _, came, keep, out, _, _, tail_came, tail_keep, tail_out, _ = buffers
-        whole(came, base).wait_recv()
-        whole(tail_came, base + 1).wait_recv()
-        out[...] = (keep[...] + came[...].astype(F32)).astype(BF16)
-        tail_out[...] = (tail_keep[...] + tail_came[...].astype(F32)).astype(BF16)
-
-    def ffw_send(buffers, base):
+        if i == 2:
+            whole(tail_came, sems[2]).wait_recv()
+            tail_out[...] = (tail_keep[...] + tail_came[...].astype(F32)).astype(BF16)
+            return
+        whole(came.at[pl.ds(0, 8)], sems[i]).wait_recv()
+        for dz in parts[i]:
+            rows = pl.ds(4 * lax.rem(z + dz, 4), 4)
+            out[rows] = (keep[rows] + came[rows].astype(F32)).astype(BF16)
+
+    def ffw_send(buffers, base, i):
         _, _, _, out, into, _, _, _, tail_out, tail_into = buffers
+        if i < 2:
+            for dz in parts[i]:
+                for dx in (2, 1, 3, 0):
+                    if dz or dx:
+                        s2 = 4 * lax.rem(z + dz, 4) + lax.rem(x + dx, 4)
+                        send(out.at[s2], into.at[s], base, {"seq": s2})
+            return
 
         def one(q, carry):
             z2 = 2 * g + lax.div(q, 2)
@@ -206,11 +232,13 @@
             return carry
 
         lax.fori_loop(0, 4, one, 0)
-        to_plane(lambda g2, s2: send(out.at[s2], into.at[s], base, {"seq": s2}), NS)
         into[s] = out[s]
         pending.append((out.at[pl.ds(0, NS - 1)], base, None))
         pending.append((tail_out.at[pl.ds(0, 3)], base + 1, holds_extra))
         pending.append((tail_out, base + 1, jnp.logical_not(holds_extra)))
+
+    sems_a = (6, 8, 7)
+    sems_b = (19, 15, 20)
 
     for load in loads[12:23]:
         load.wait()
@@ -298,7 +326,7 @@
 
     loads[8].wait()
     loads[9].wait()
-    ffw_product(x_in * gain2[...], set_a, 6)
+    ffw_product(x_in * gain2[...], set_a, sems_a)
     for i in range(3, 7):
         loads[i].wait()
     whole(b2.at[pl.ds(0, NP - 1)], 1).wait_recv()
@@ -351,7 +379,8 @@
             ks[k * 8 + j] = kx[j * 8:(j + 1) * 8, :]
             vs[k * 8 + j] = vx[j * 8:(j + 1) * 8, :]
 
-    ffw_combine(set_a, 6)
+    for i in range(3):
+        ffw_combine(set_a, sems_a, i)
     loads[11].wait()
     pick_table(0, 1)
 
@@ -392,20 +421,24 @@
     b5[kv] = nt_dot(att, w_o[...])
     to_kv(lambda k2: send(b5.at[kv], b5.at[kv], 4, {"kv": k2}))
     pending.append((b5.at[pl.ds(0, NKV - 1)], 4, None))
-    ffw_send(set_a, 17)
+    for i in range(3):
+        ffw_send(set_a, 17, i)
     pick_table(3, 1)
     whole(b5.at[pl.ds(0, NKV - 1)], 4).wait_recv()
     projected = (b5[0] + b5[1]) + (b5[2] + b5[3])
     branch = projected * gain1[...]
-    ffw_product(branch * gain2[...], set_b, 19)
+    ffw_product(branch * gain2[...], set_b, sems_b)
+    ffw_combine(set_b, sems_b, 0)
+    ffw_send(set_b, 21, 0)
     b6[me, 0:1, :] = column_to_row(jnp.sum(projected * projected, axis=-1, keepdims=True))
     b6[me, 1:2, :] = column_to_row(jnp.sum(x_in * branch, axis=-1, keepdims=True))
     b6[me, 2:3, :] = column_to_row(jnp.sum(branch * branch, axis=-1, keepdims=True))
     b6[me, 3:4, :] = x_sq
     to_plane(lambda g2, s2: send(b6.at[me], b6.at[me], 5, {"guide": g2, "seq": s2}))
     pending.append((b6.at[pl.ds(0, NP - 1)], 5, None))
-    ffw_combine(set_b, 19)
-    ffw_send(set_b, 21)
+    for i in range(1, 3):
+        ffw_combine(set_b, sems_b, i)
+        ffw_send(set_b, 21, i)
     pick_table(4, 3)
     whole(b6.at[pl.ds(0, NP - 1)], 5).wait_recv()
     sums = jnp.sum(b6[...], axis=0)

time: 65.3 us -> 65.2 us (level)
  no operation moved by 1% of the time
where the time goes in v6:
time: 65.2 us; the launch traced here: 64.9 us
  Pallas kernels  63.6 us (98%)
  other arithmetic  1.35 us (2%)
    pallas_call x1, Pallas kernels, on_device(): pl.pallas_call(step_kernel, out_shape=[jax.ShapeDtypeStruct((4, PICK), F3...  63.6 us
    add x1, other arithmetic, on_device(): return base + lift  1.35 us

profile of v6, /device:TPU:1, one launch (start us, length us, event | category | flops | bytes accessed | tf_op | source)
XLA Modules:
  0.0 64.9 jit_solution(3549857810797860830)
XLA Ops:
  0.0 63.6 %decode_step.1 = (f32[4,1024]{1,0:T(4,128)}, f32[4,1024]{1,0:T(4,128)}) custom-call(s32[2,8]{1,0:T(2,128)} %lengths_h.1, s32[2,8]{1,0:T(2,128)} %owner_h.1, f32[8]{0:T(128)} %guidance_h.1, bf16[2,8,144]{2,1,0:T(8,128)(2,1)} %hidden_h.1, s32[8,128]{1,0:T(8,128)} %bitcast.10, f32[1,128]{1,0:T(1,128)} %constant.2.clone.freq_h, f32[1,144]{1,0:T(1,128)} %bitcast.11, ...), custom_call_target="tpu_custom_call" | custom-call | tf_op jit(solution)/shard_map/decode_step/pallas_call | solution.py:571
  63.6 1.3 %add.3 = f32[4,1024]{1,0:T(4,128)} add(f32[4,1024]{1,0:T(4,128)} %get-tuple-element.7, f32[4,1024]{1,0:T(4,128)} %get-tuple-element.8) | non-fusion elementwise | flops 4096 | bytes 49152 | tf_op jit(solution)/shard_map/add | solution.py:644
